TPU v7x, 512 devices: a whole 4x8x8 slice. The times are simulated.
512 devices in a mesh: pair: 64 (over z_hi, y, core), tm: 8 (over x, z_lo).
Axes of the slice: x: 4, y: 8, z: 8 (z_hi: 4, z_lo: 2; z = z_hi * 2 + z_lo), core: 2. Of those that a mesh axis runs over, the one named last changes fastest.
Arguments:
- raw: bfloat16 [8, 16384, 128], P('tm', 'pair'), may hold values from -60 to 60
- valid: int32 [8, 16384], P('tm', 'pair'), may hold values 0 or 1
Outputs:
- near_corr: float32 [16384, 4096], P('pair', 'tm')
- far_corr: float32 [16384, 4096], P('pair', 'tm')
All inputs are finite; a program needn't handle non-finite values. No bound on the sum of `valid` on one device may be relied on, other than what follows from the above.
Results may differ from a plain program's by a relative error of at most 0.014.
Values may be sent and summed in bfloat16 or wider, within the bound.
No kernel may reach another device: no remote copies, remote signals or barrier semaphores. Data moves between devices by JAX's collectives and lax.ppermute only.
A program may use at most 64 MiB of HBM per device.

v0:
```python
import math

import jax
import jax.numpy as jnp
from jax import lax
from jax.sharding import PartitionSpec as P

LAGS = 16


def shifted(value, axis, steps):
    count = lax.axis_size(axis)
    pairs = [(source, (source + steps) % count) for source in range(count)]
    return lax.ppermute(value, axis, pairs)


def make_basis(samples, freqs):
    times = jnp.arange(samples, dtype=jnp.float32)[:, None]
    bins = jnp.arange(freqs, dtype=jnp.float32)[None, :]
    hann = 0.5 - 0.5 * jnp.cos(2.0 * math.pi * times / samples)
    angle = 2.0 * math.pi * bins * times / samples
    return jnp.concatenate([hann * jnp.cos(angle), -hann * jnp.sin(angle)], axis=1).astype(
        jnp.bfloat16
    )


def lag_tables(lags, freqs, samples):
    shift_lag = jnp.arange(lags, dtype=jnp.float32)[:, None] - lags // 2
    bins = jnp.arange(freqs, dtype=jnp.float32)[None, :]
    theta = 2.0 * math.pi * bins * shift_lag / samples
    return (jnp.cos(theta).astype(jnp.bfloat16), jnp.sin(theta).astype(jnp.bfloat16))


def correlate(own, other, cos_table, sin_table, freqs, scale):
    windows, chans, _ = own.shape
    lags = cos_table.shape[0]
    cos_wide = jnp.transpose(cos_table.astype(jnp.float32))[None, :, :, None]
    sin_wide = jnp.transpose(sin_table.astype(jnp.float32))[None, :, :, None]
    step = min(windows, 4)
    count = min(step, windows)
    oth_re = jnp.transpose(other[:, :, :freqs], (0, 2, 1)).astype(jnp.float32)[:, :, None, :]
    oth_im = jnp.transpose(other[:, :, freqs:], (0, 2, 1)).astype(jnp.float32)[:, :, None, :]
    mod_a = cos_wide * oth_re + sin_wide * oth_im
    mod_b = cos_wide * oth_im - sin_wide * oth_re
    modded = (
        jnp.stack([mod_a, mod_b], axis=1)
        .astype(jnp.bfloat16)
        .reshape(count * 2 * freqs, lags * chans)
    )
    left = jnp.transpose(own, (1, 0, 2)).reshape(chans, count * 2 * freqs)
    total = jnp.dot(left, modded, preferred_element_type=jnp.float32)
    return (total * scale).astype(jnp.bfloat16)


def local(raw, valid):
    windows, chans, samples = raw.shape
    freqs = samples // 2
    scale = 1.0 / math.sqrt(windows * lax.axis_size("tm") * freqs)
    basis = make_basis(samples, freqs)
    cos_table, sin_table = lag_tables(LAGS, freqs, samples)
    spectra = jnp.dot(
        raw.reshape(windows * chans, samples), basis, preferred_element_type=jnp.float32
    )
    spectra = spectra.reshape(windows, chans, 2 * freqs)
    power = jnp.mean(spectra * spectra, axis=-1, keepdims=True) + 1e-06
    white = (spectra * lax.rsqrt(power) * valid[..., None].astype(jnp.float32)).astype(jnp.bfloat16)
    near_white = shifted(white, "pair", -1)
    far_white = shifted(white, "pair", -2)
    near_part = correlate(white, near_white, cos_table, sin_table, freqs, scale)
    near_corr = lax.psum_scatter(
        near_part.astype(jnp.float32).astype(jnp.bfloat16), "tm", scatter_dimension=1, tiled=True
    ).astype(jnp.float32)
    far_part = correlate(white, far_white, cos_table, sin_table, freqs, scale)
    far_corr = lax.psum_scatter(
        far_part.astype(jnp.float32).astype(jnp.bfloat16), "tm", scatter_dimension=1, tiled=True
    ).astype(jnp.float32)
    return (near_corr, far_corr)


def solution(mesh):
    return jax.shard_map(
        local,
        mesh=mesh,
        in_specs=(P("tm", "pair", None), P("tm", "pair")),
        out_specs=(P("pair", "tm"), P("pair", "tm")),
        check_vma=False,
    )
```

profile of v0, /device:TPU:1, one launch (start us, length us, event | category | flops | bytes accessed | tf_op | source)
XLA Modules:
  0.0 153.5 jit_solution(17651827808095855980)
XLA Ops:
  7.2 0.0 copy-start
  7.2 0.0 reduce-scatter.5.cloned.1.call-start
  7.3 0.7 convert_element_type.133
  8.0 0.2 multiply_convert_fusion.2
  8.2 0.0 copy-done
  8.2 0.2 multiply_reduce_fusion
  8.4 14.4 %collective-permute-start.1 = (bf16[1,256,128]{1,2,0:T(8,128)(2,1)S(1)}, bf16[1,256,128]{1,2,0:T(8,128)(2,1)S(1)}, u32[]{:S(2)}, u32[]{:S(2)}) collective-permute-start(bf16[1,256,128]{1,2,0:T(8,128)(2,1)S(1)} %fusion.15), channel_id=1, source_target_pairs={{0,496},{8,504},{16,0},{24,8},{32,16},{40,24},{48,32},{56,40},{64,... | collective-permute-start | bytes 196616 | tf_op jit(solution)/shard_map/ppermute | solution.py:14
  22.8 2.9 %collective-permute-start = (bf16[1,256,128]{1,2,0:T(8,128)(2,1)S(1)}, bf16[1,256,128]{1,2,0:T(8,128)(2,1)S(1)}, u32[]{:S(2)}, u32[]{:S(2)}) collective-permute-start(bf16[1,256,128]{1,2,0:T(8,128)(2,1)S(1)} %fusion.15), channel_id=1, source_target_pairs={{0,504},{8,0},{16,8},{24,16},{32,24},{40,32},{48,40},{56,48},{64,5... | collective-permute-start | bytes 196616 | tf_op jit(solution)/shard_map/ppermute | solution.py:14
  25.7 0.1 fusion.7
  25.8 0.1 copy.4
  25.9 0.1 copy.5
  26.0 0.0 collective-permute-done.1
  26.0 2.4 %collective-permute-done = bf16[1,256,128]{1,2,0:T(8,128)(2,1)S(1)} collective-permute-done((bf16[1,256,128]{1,2,0:T(8,128)(2,1)S(1)}, bf16[1,256,128]{1,2,0:T(8,128)(2,1)S(1)}, u32[]{:S(2)}, u32[]{:S(2)}) %collective-permute-start) | collective-permute-done | bytes 65568 | tf_op jit(solution)/shard_map/ppermute | solution.py:14
  28.4 0.6 add_convert_fusion
  29.0 0.1 pad_maximum_fusion.1
  29.1 0.4 copy.7
  29.5 2.0 %fusion.1 = bf16[256,4096]{1,0:T(8,128)(2,1)} fusion(bf16[128,4096]{1,0:T(8,128)(2,1)S(1)} %bitcast.39, f32[128,256]{1,0:T(8,128)S(1)} %get-tuple-element.17, f32[256]{0:T(256)S(1)} %bitcast.41, f32[256]{0:T(256)S(1)} %add_rsqrt_fusion), kind=kOutput, calls=%fused_computation.3 | convolution fusion | flops 270630912 | bytes 3278848 | tf_op jit(solution)/shard_map/dot_general | solution.py:51
  31.6 0.0 reduce-scatter.5.cloned.1.call-update
  31.6 0.0 reduce-scatter.3.cloned.1.call-start
  31.6 0.1 pad_maximum_fusion
  31.7 0.4 copy.6
  32.2 2.1 %fusion = bf16[256,4096]{1,0:T(8,128)(2,1)} fusion(bf16[128,4096]{1,0:T(8,128)(2,1)S(1)} %bitcast.38, f32[128,256]{1,0:T(8,128)S(1)} %get-tuple-element.17, f32[256]{0:T(256)S(1)} %bitcast.42, f32[256]{0:T(256)S(1)} %add_rsqrt_fusion), kind=kOutput, calls=%fused_computation.2 | convolution fusion | flops 270630912 | bytes 3278848 | tf_op jit(solution)/shard_map/dot_general | solution.py:51
  34.3 0.0 reduce-scatter.3.cloned.1.call-update
  34.3 50.5 %reduce-scatter.5.cloned.1.call-done = bf16[256,512]{1,0:T(8,128)(2,1)} async-done(((bf16[256,4096]{1,0:T(8,128)(2,1)}), bf16[256,512]{1,0:T(8,128)(2,1)}) %reduce-scatter.5.cloned.1.call-update) | async-done | bytes 262160 | tf_op jit(solution)/shard_map/reduce_scatter | solution.py:74
  84.8 1.8 %convert_element_type.151 = f32[256,512]{1,0:T(8,128)} convert(bf16[256,512]{1,0:T(8,128)(2,1)} %reduce-scatter.5.cloned.1.call-done) | non-fusion elementwise | flops 131072 | bytes 786432 | tf_op jit(solution)/shard_map/convert_element_type | solution.py:76
  86.6 58.2 %reduce-scatter.3.cloned.1.call-done = bf16[256,512]{1,0:T(8,128)(2,1)} async-done(((bf16[256,4096]{1,0:T(8,128)(2,1)}), bf16[256,512]{1,0:T(8,128)(2,1)}) %reduce-scatter.3.cloned.1.call-update) | async-done | bytes 262160 | tf_op jit(solution)/shard_map/reduce_scatter | solution.py:70
  144.8 1.8 %convert_element_type.146 = f32[256,512]{1,0:T(8,128)} convert(bf16[256,512]{1,0:T(8,128)(2,1)} %reduce-scatter.3.cloned.1.call-done) | non-fusion elementwise | flops 131072 | bytes 786432 | tf_op jit(solution)/shard_map/convert_element_type | solution.py:72
  (7 shorter events, 0.1 us)
Async XLA Ops:
  7.2 1.0 copy-start
  7.2 77.6 %reduce-scatter.5.cloned.1.call-start = ((), (), s32[]{:S(2)}) async-start(), calls=%async_computation.3 | async-start | bytes 2359296 | tf_op jit(solution)/shard_map/reduce_scatter | solution.py:74
  8.4 17.6 %collective-permute-start.1 = (bf16[1,256,128]{1,2,0:T(8,128)(2,1)S(1)}, bf16[1,256,128]{1,2,0:T(8,128)(2,1)S(1)}, u32[]{:S(2)}, u32[]{:S(2)}) collective-permute-start(bf16[1,256,128]{1,2,0:T(8,128)(2,1)S(1)} %fusion.15), channel_id=1, source_target_pairs={{0,496},{8,504},{16,0},{24,8},{32,16},{40,24},{48,32},{56,40},{64,... | collective-permute-start | bytes 196616 | tf_op jit(solution)/shard_map/ppermute | solution.py:14
  22.8 5.6 %collective-permute-start = (bf16[1,256,128]{1,2,0:T(8,128)(2,1)S(1)}, bf16[1,256,128]{1,2,0:T(8,128)(2,1)S(1)}, u32[]{:S(2)}, u32[]{:S(2)}) collective-permute-start(bf16[1,256,128]{1,2,0:T(8,128)(2,1)S(1)} %fusion.15), channel_id=1, source_target_pairs={{0,504},{8,0},{16,8},{24,16},{32,24},{40,32},{48,40},{56,48},{64,5... | collective-permute-start | bytes 196616 | tf_op jit(solution)/shard_map/ppermute | solution.py:14
  31.6 113.2 %reduce-scatter.3.cloned.1.call-start = ((), (), s32[]{:S(2)}) async-start(), calls=%async_computation.2 | async-start | bytes 2359296 | tf_op jit(solution)/shard_map/reduce_scatter | solution.py:70
Sparse Core Ops, SparseCore 0:
  31.7 53.0 reduce-scatter.4
  87.7 57.1 reduce-scatter.2
where the time goes:
time: 154 us; the launch traced here: 153 us
  waiting for transfers between devices  111 us (72%)
  starting transfers between devices  17.3 us (11%)
  between operations  14.2 us (9%)
  other arithmetic  5.49 us (4%)
  matrix products  4.32 us (3%)
    reduce_scatter x1, waiting for transfers between devices, local(): lax.psum_scatter(near_part.astype(jnp.float32).astype(jnp.bfloat16), 'tm'...  58.2 us
    reduce_scatter x1, waiting for transfers between devices, local(): lax.psum_scatter(far_part.astype(jnp.float32).astype(jnp.bfloat16), 'tm',...  50.5 us
    ppermute x2, starting transfers between devices, shifted(): return lax.ppermute(value, axis, pairs)  17.2 us
    dot_general x2, matrix products, correlate(): total = jnp.dot(left, modded, preferred_element_type=jnp.float32)  4.13 us
  transfers between devices with their start and end apart: 4, of which 3 were waited for; matrix products, arithmetic and copies ran while one was open for 3% of the time, Pallas kernels for 0%

commit v1 on v0

v1 whole, which is shorter than its diff:
```python
import math

import jax
import jax.numpy as jnp
from jax import lax
from jax.experimental import pallas as pl
from jax.experimental.pallas import tpu as pltpu
from jax.sharding import PartitionSpec as P

LAGS = 16


def make_basis(samples, freqs):
    times = jnp.arange(samples, dtype=jnp.float32)[:, None]
    bins = jnp.arange(freqs, dtype=jnp.float32)[None, :]
    hann = 0.5 - 0.5 * jnp.cos(2.0 * math.pi * times / samples)
    angle = 2.0 * math.pi * bins * times / samples
    return jnp.concatenate([hann * jnp.cos(angle), -hann * jnp.sin(angle)], axis=1).astype(
        jnp.bfloat16
    )


def lag_tables(first, lags, freqs, samples):
    shift_lag = (first + jnp.arange(lags) - LAGS // 2).astype(jnp.float32)[:, None]
    bins = jnp.arange(freqs, dtype=jnp.float32)[None, :]
    theta = 2.0 * math.pi * bins * shift_lag / samples
    cos = jnp.cos(theta).astype(jnp.bfloat16).astype(jnp.float32)
    sin = jnp.sin(theta).astype(jnp.bfloat16).astype(jnp.float32)
    return jnp.concatenate([cos, cos], axis=1), jnp.concatenate([-sin, sin], axis=1)


def in_vmem(value):
    return pltpu.with_memory_space_constraint(value, pltpu.VMEM)


def rotated(own, cos, sin):
    wide = own.astype(jnp.float32)
    swapped = pltpu.roll(wide, wide.shape[-1] // 2, 1)
    return (wide * cos + swapped * sin).astype(jnp.bfloat16)


def far_kernel(odd_ref, gath_ref, cos_ref, sin_ref, out_ref, mod_ref, *, scale):
    windows, both, width = gath_ref.shape
    chans = both // 2
    lag = pl.program_id(0)
    odd = odd_ref[0]
    own_at = pl.multiple_of(odd * chans, chans)
    far_at = pl.multiple_of((1 - odd) * chans, chans)
    rows = pl.multiple_of(lag * chans, chans)
    cos = cos_ref[pl.ds(lag, 1), :]
    sin = sin_ref[pl.ds(lag, 1), :]
    for w in range(windows):
        own = gath_ref[w, pl.ds(own_at, chans), :]
        mod_ref[pl.ds(rows, chans), w * width : (w + 1) * width] = rotated(own, cos, sin)
    other = jnp.concatenate(
        [gath_ref[w, pl.ds(far_at, chans), :] for w in range(windows)], axis=1
    )
    total = lax.dot_general(
        mod_ref[pl.ds(rows, chans), :], other, (((1,), (1,)), ((), ())), preferred_element_type=jnp.float32
    )
    out_ref[...] = total * scale


def near_kernel(mod_ref, other_ref, out_ref, *, scale):
    windows, chans, _ = other_ref.shape
    lag = pl.program_id(0)
    other = jnp.concatenate([other_ref[w] for w in range(windows)], axis=1)
    rows = pl.multiple_of(lag * chans, chans)
    total = lax.dot_general(
        mod_ref[pl.ds(rows, chans), :], other, (((1,), (1,)), ((), ())), preferred_element_type=jnp.float32
    )
    out_ref[...] = total * scale


def local(raw, valid):
    windows, chans, samples = raw.shape
    freqs = samples // 2
    groups = lax.axis_size("tm")
    pairs = lax.axis_size("pair")
    total = windows * groups
    lags = LAGS // groups
    scale = 1.0 / math.sqrt(total * freqs)
    basis = make_basis(samples, freqs)
    cos, sin = lag_tables(lax.axis_index("tm") * lags, lags, freqs, samples)
    odd = (lax.axis_index("pair") % 2).astype(jnp.int32)
    spectra = jnp.dot(
        raw.reshape(windows * chans, samples), basis, preferred_element_type=jnp.float32
    )
    spectra = spectra.reshape(windows, chans, 2 * freqs)
    power = jnp.mean(spectra * spectra, axis=-1, keepdims=True) + 1e-06
    white = (spectra * lax.rsqrt(power) * valid[..., None].astype(jnp.float32)).astype(jnp.bfloat16)

    far = lax.ppermute(white, "pair", [(p, (p - 2) % pairs) for p in range(pairs)])
    is_odd = odd == 1
    slots = jnp.concatenate([jnp.where(is_odd, far, white), jnp.where(is_odd, white, far)], axis=1)
    sends = jnp.broadcast_to(slots[None], (groups, windows, 2 * chans, samples))
    gathered = lax.all_to_all(
        sends.reshape(total, 2 * chans, samples), "tm", 0, 0, tiled=True
    )
    near = lax.ppermute(gathered[:, chans:, :], "pair", [(p, p ^ 1) for p in range(pairs)])

    vmem = pl.BlockSpec(memory_space=pltpu.VMEM)
    far_corr, mod = pl.pallas_call(
        lambda *refs: far_kernel(*refs, scale=scale),
        grid=(lags,),
        in_specs=[
            pl.BlockSpec(memory_space=pltpu.SMEM),
            vmem,
            vmem,
            vmem,
        ],
        out_specs=[
            pl.BlockSpec((chans, chans), lambda l: (0, l)),
            vmem,
        ],
        out_shape=[
            jax.ShapeDtypeStruct((chans, lags * chans), jnp.float32),
            pltpu.VMEM((lags * chans, total * samples), jnp.bfloat16),
        ],
        name="far_corr",
    )(odd.reshape(1), in_vmem(gathered), in_vmem(cos), in_vmem(sin))
    near_corr = pl.pallas_call(
        lambda *refs: near_kernel(*refs, scale=scale),
        grid=(lags,),
        in_specs=[
            vmem,
            vmem,
        ],
        out_specs=pl.BlockSpec((chans, chans), lambda l: (0, l)),
        out_shape=jax.ShapeDtypeStruct((chans, lags * chans), jnp.float32),
        name="near_corr",
    )(mod, in_vmem(near))
    return (near_corr, far_corr)


def solution(mesh):
    return jax.shard_map(
        local,
        mesh=mesh,
        in_specs=(P("tm", "pair", None), P("tm", "pair")),
        out_specs=(P("pair", "tm"), P("pair", "tm")),
        check_vma=False,
    )
```

time: 154 us -> 48.7 us (0.32)
  waiting for transfers between devices: 111 us -> 15.3 us
  between operations: 14.2 us -> 0.73 us
  starting transfers between devices: 17.3 us -> 23.9 us
  other arithmetic: 5.49 us -> 0.6 us
  Pallas kernels: 0 us -> 4.24 us
  matrix products: 4.32 us -> 0.19 us
  local copies, waits for them, and re-layouts: 1.02 us -> 3.47 us
    reduce_scatter x2 -> x0, waiting for transfers between devices: 109 us -> none  [the longest x1 58.2 us: local(): lax.psum_scatter(near_part.astype(jnp.float32).astype(jnp.bfloat16), 'tm'...]
    all_to_all x0 -> x1, waiting for transfers between devices: none -> 14 us  [local(): lax.all_to_all(sends.reshape(total, 2 * chans, samples), 'tm', 0, 0, tile...]
    all_to_all x0 -> x1, starting transfers between devices: none -> 4.93 us  [local(): lax.all_to_all(sends.reshape(total, 2 * chans, samples), 'tm', 0, 0, tile...]
    pallas_call x0 -> x2, Pallas kernels: none -> 4.24 us  [the longest x1 2.62 us: local(): pl.pallas_call(lambda *refs: near_kernel(*refs, scale=scale), grid=(lags,...]
    dot_general x2 -> x0, matrix products: 4.13 us -> none  [correlate(): total = jnp.dot(left, modded, preferred_element_type=jnp.float32)]
    convert_element_type x3 -> x1, other arithmetic: 3.72 us -> 0.01 us  [lag_tables(): (first + jnp.arange(lags) - LAGS // 2).astype(jnp.float32)[:, None]]
    ppermute x2, starting transfers between devices: 17.2 us -> 19 us  [the longest x1 14.4 us: local(): lax.ppermute(white, 'pair', [(p, (p - 2) % pairs) for p in range(pairs)])]
  transfers between devices with their start and end apart: 4 -> 3, of which waited for: 3 -> 2; matrix products, arithmetic and copies ran while one was open for 3% -> 1% of each run, Pallas kernels for 0% -> 3%
where the time goes in v1:
time: 48.7 us; the launch traced here: 48.4 us
  starting transfers between devices  23.9 us (49%)
  waiting for transfers between devices  15.3 us (31%)
  Pallas kernels  4.24 us (9%)
  local copies, waits for them, and re-layouts  3.47 us (7%)
  between operations  0.73 us (1%)
  other arithmetic  0.6 us (1%)
    ppermute x1, starting transfers between devices, local(): lax.ppermute(white, 'pair', [(p, (p - 2) % pairs) for p in range(pairs)])  14.4 us
    all_to_all x1, waiting for transfers between devices, local(): lax.all_to_all(sends.reshape(total, 2 * chans, samples), 'tm', 0, 0, tile...  14 us
    all_to_all x1, starting transfers between devices, local(): lax.all_to_all(sends.reshape(total, 2 * chans, samples), 'tm', 0, 0, tile...  4.93 us
    ppermute x1, starting transfers between devices, local(): lax.ppermute(gathered[:, chans:, :], 'pair', [(p, p ^ 1) for p in range(p...  4.57 us
    pallas_call x1, Pallas kernels, local(): pl.pallas_call(lambda *refs: near_kernel(*refs, scale=scale), grid=(lags,...  2.62 us
    unnamed x6, local copies, waits for them, and re-layouts  2.2 us
    pallas_call x1, Pallas kernels, local(): pl.pallas_call(lambda *refs: far_kernel(*refs, scale=scale), grid=(lags,)...  1.63 us
    ppermute x1, waiting for transfers between devices, local(): lax.ppermute(white, 'pair', [(p, (p - 2) % pairs) for p in range(pairs)])  1.3 us
  transfers between devices with their start and end apart: 3, of which 2 were waited for; matrix products, arithmetic and copies ran while one was open for 1% of the time, Pallas kernels for 3%

profile of v1, /device:TPU:1, one launch (start us, length us, event | category | flops | bytes accessed | tf_op | source)
XLA Modules:
  0.0 48.4 jit_solution(10814139327040570111)
XLA Ops:
  0.6 0.0 copy-start
  0.7 0.2 multiply_convert_fusion.2
  0.9 0.6 %copy-done = bf16[1,256,128]{2,1,0:T(8,128)(2,1)S(1)} copy-done((bf16[1,256,128]{2,1,0:T(8,128)(2,1)S(1)}, bf16[1,256,128]{2,1,0:T(8,128)(2,1)}, u32[]{:S(2)}) %copy-start) | copy-done | bytes 65560
  1.5 0.2 multiply_reduce_fusion
  1.7 0.0 copy-start.2
  1.7 0.7 %copy-done.2 = s32[1,256]{1,0:T(1,128)S(1)} copy-done((s32[1,256]{1,0:T(1,128)S(1)}, s32[1,256]{1,0:T(1,128)}, u32[]{:S(2)}) %copy-start.2) | copy-done | bytes 1048
  2.4 14.4 %collective-permute-start = (bf16[1,256,128]{1,2,0:T(8,128)(2,1)S(1)}, bf16[1,256,128]{1,2,0:T(8,128)(2,1)S(1)}, u32[]{:S(2)}, u32[]{:S(2)}) collective-permute-start(bf16[1,256,128]{1,2,0:T(8,128)(2,1)S(1)} %fusion), channel_id=1, source_target_pairs={{0,496},{8,504},{16,0},{24,8},{32,16},{40,24},{48,32},{56,40},{64,... | collective-permute-start | bytes 196616 | tf_op jit(solution)/shard_map/ppermute | solution.py:93
  16.8 1.3 %collective-permute-done = bf16[1,256,128]{1,2,0:T(8,128)(2,1)S(1)} collective-permute-done((bf16[1,256,128]{1,2,0:T(8,128)(2,1)S(1)}, bf16[1,256,128]{1,2,0:T(8,128)(2,1)S(1)}, u32[]{:S(2)}, u32[]{:S(2)}) %collective-permute-start) | collective-permute-done | bytes 65568 | tf_op jit(solution)/shard_map/ppermute | solution.py:93
  18.1 0.1 copy.5
  18.2 1.1 %reshape.72 = bf16[8,512,128]{2,1,0:T(8,128)(2,1)} broadcast(bf16[512,128]{1,0:T(8,128)(2,1)S(1)} %copy.5), dimensions={1,2} | broadcast | bytes 1179648 | tf_op jit(solution)/shard_map/reshape | solution.py:98
  19.4 4.9 %all-to-all-start = ((bf16[8,512,128]{2,1,0:T(8,128)(2,1)}), bf16[8,512,128]{2,1,0:T(8,128)(2,1)S(1)}, u32[]{:S(2)}, u32[]{:S(2)}) async-start(bf16[8,512,128]{2,1,0:T(8,128)(2,1)} %reshape.72), calls=%async_computation | async-start | bytes 2097152 | tf_op jit(solution)/shard_map/all_to_all | solution.py:97
  24.3 14.0 %all-to-all-done.refs_1_ = bf16[8,512,128]{2,1,0:T(8,128)(2,1)S(1)} async-done(((bf16[8,512,128]{2,1,0:T(8,128)(2,1)}), bf16[8,512,128]{2,1,0:T(8,128)(2,1)S(1)}, u32[]{:S(2)}, u32[]{:S(2)}) %all-to-all-start) | async-done | bytes 1048608 | tf_op jit(solution)/shard_map/all_to_all | solution.py:97
  38.3 4.6 %collective-permute-start.1 = (bf16[8,256,128]{2,1,0:T(8,128)(2,1)S(1)}, bf16[8,256,128]{2,1,0:T(8,128)(2,1)S(1)}, u32[]{:S(2)}, u32[]{:S(2)}) collective-permute-start(bf16[8,256,128]{2,1,0:T(8,128)(2,1)S(1)} %slice.4), channel_id=1, source_target_pairs={{0,8},{8,0},{16,24},{24,16},{32,40},{40,32},{48,56},{56,48},{64,72... | collective-permute-start | bytes 1572872 | tf_op jit(solution)/shard_map/ppermute | solution.py:100
  42.9 0.1 fusion.9
  43.0 0.1 maximum_convert_fusion.refs_2_
  43.1 0.1 pad_maximum_fusion.refs_3_
  43.2 1.6 %far_corr.1 = (f32[256,512]{1,0:T(8,128)}, bf16[512,1024]{1,0:T(8,128)(2,1)S(1)}) custom-call(s32[1]{0:T(128)} %bitcast.refs_0_, bf16[8,512,128]{2,1,0:T(8,128)(2,1)S(1)} %all-to-all-done.refs_1_, f32[2,128]{1,0:T(2,128)S(1)} %maximum_convert_fusion.refs_2_, f32[2,128]{1,0:T(2,128)S(1)} %pad_maximum_fusion.refs_3_), custom_call_target="tpu_custom_call" | custom-call | tf_op jit(solution)/shard_map/far_corr/pallas_call | solution.py:103
  44.8 0.0 copy-start.1
  44.8 1.0 %copy-done.1 = bf16[512,1024]{1,0:T(8,128)(2,1)} copy-done((bf16[512,1024]{1,0:T(8,128)(2,1)}, bf16[512,1024]{1,0:T(8,128)(2,1)S(1)}, u32[]{:S(2)}) %copy-start.1) | copy-done | bytes 1048600
  45.8 0.0 collective-permute-done.1.refs_1_
  45.8 2.6 %near_corr.1 = f32[256,512]{1,0:T(8,128)} custom-call(bf16[512,1024]{1,0:T(8,128)(2,1)} %copy-done.1, bf16[8,256,128]{2,1,0:T(8,128)(2,1)S(1)} %collective-permute-done.1.refs_1_), custom_call_target="tpu_custom_call" | custom-call | tf_op jit(solution)/shard_map/near_corr/pallas_call | solution.py:122
  (9 shorter events, 0.2 us)
Async XLA Ops:
  0.6 0.8 %copy-start = (bf16[1,256,128]{2,1,0:T(8,128)(2,1)S(1)}, bf16[1,256,128]{2,1,0:T(8,128)(2,1)}, u32[]{:S(2)}) copy-start(bf16[1,256,128]{2,1,0:T(8,128)(2,1)} %param.2) | copy-start | bytes 196612
  1.7 0.7 %copy-start.2 = (s32[1,256]{1,0:T(1,128)S(1)}, s32[1,256]{1,0:T(1,128)}, u32[]{:S(2)}) copy-start(s32[1,256]{1,0:T(1,128)} %param.3) | copy-start | bytes 3076
  2.4 15.7 %collective-permute-start = (bf16[1,256,128]{1,2,0:T(8,128)(2,1)S(1)}, bf16[1,256,128]{1,2,0:T(8,128)(2,1)S(1)}, u32[]{:S(2)}, u32[]{:S(2)}) collective-permute-start(bf16[1,256,128]{1,2,0:T(8,128)(2,1)S(1)} %fusion), channel_id=1, source_target_pairs={{0,496},{8,504},{16,0},{24,8},{32,16},{40,24},{48,32},{56,40},{64,... | collective-permute-start | bytes 196616 | tf_op jit(solution)/shard_map/ppermute | solution.py:93
  19.4 18.9 %all-to-all-start = ((bf16[8,512,128]{2,1,0:T(8,128)(2,1)}), bf16[8,512,128]{2,1,0:T(8,128)(2,1)S(1)}, u32[]{:S(2)}, u32[]{:S(2)}) async-start(bf16[8,512,128]{2,1,0:T(8,128)(2,1)} %reshape.72), calls=%async_computation | async-start | bytes 2097152 | tf_op jit(solution)/shard_map/all_to_all | solution.py:97
  38.3 7.5 %collective-permute-start.1 = (bf16[8,256,128]{2,1,0:T(8,128)(2,1)S(1)}, bf16[8,256,128]{2,1,0:T(8,128)(2,1)S(1)}, u32[]{:S(2)}, u32[]{:S(2)}) collective-permute-start(bf16[8,256,128]{2,1,0:T(8,128)(2,1)S(1)} %slice.4), channel_id=1, source_target_pairs={{0,8},{8,0},{16,24},{24,16},{32,40},{40,32},{48,56},{56,48},{64,72... | collective-permute-start | bytes 1572872 | tf_op jit(solution)/shard_map/ppermute | solution.py:100
  44.8 1.0 %copy-start.1 = (bf16[512,1024]{1,0:T(8,128)(2,1)}, bf16[512,1024]{1,0:T(8,128)(2,1)S(1)}, u32[]{:S(2)}) copy-start(bf16[512,1024]{1,0:T(8,128)(2,1)S(1)} %get-tuple-element.4.refs_0_) | copy-start | bytes 3145732

commit v2 on v0

v2 whole, which is shorter than its diff:
```python
import functools
import math

import jax
import jax.numpy as jnp
import numpy as np
from jax import lax
from jax.experimental import pallas as pl
from jax.experimental.pallas import tpu as pltpu
from jax.sharding import PartitionSpec as P

LAGS = 16


def make_basis(samples, freqs):
    times = np.arange(samples, dtype=np.float64)[:, None]
    bins = np.arange(freqs, dtype=np.float64)[None, :]
    hann = 0.5 - 0.5 * np.cos(2.0 * math.pi * times / samples)
    angle = 2.0 * math.pi * bins * times / samples
    return np.concatenate([hann * np.cos(angle), -hann * np.sin(angle)], axis=1).astype(
        jnp.bfloat16
    )


def lag_tables(lags, freqs, samples):
    shift_lag = np.arange(lags, dtype=np.float64)[:, None] - lags // 2
    bins = np.arange(freqs, dtype=np.float64)[None, :]
    theta = 2.0 * math.pi * bins * shift_lag / samples
    cos = np.cos(theta).astype(jnp.bfloat16).astype(np.float32)
    sin = np.sin(theta).astype(jnp.bfloat16).astype(np.float32)
    return np.concatenate([cos, cos, -sin, sin], axis=1)


def in_vmem(value):
    return pltpu.with_memory_space_constraint(value, pltpu.VMEM)


VMEM_SPEC = pl.BlockSpec(memory_space=pltpu.VMEM)


def on_chip(kernel, name, out, *args, scalars=()):
    return pl.pallas_call(
        kernel,
        in_specs=[pl.BlockSpec(memory_space=pltpu.SMEM)] * len(scalars) + [VMEM_SPEC] * len(args),
        out_specs=jax.tree.map(lambda _: VMEM_SPEC, out),
        out_shape=out,
        name=name,
    )(*[jnp.reshape(scalar, (1,)) for scalar in scalars], *[in_vmem(arg) for arg in args])


def whiten_kernel(raw_hbm, valid_hbm, basis_hbm, white_ref, send_ref, raw_ref, valid_ref, basis_ref, sems):
    pairs = ((raw_hbm, raw_ref), (basis_hbm, basis_ref), (valid_hbm, valid_ref))
    loads = [pltpu.make_async_copy(src, dst, sems.at[i]) for i, (src, dst) in enumerate(pairs)]
    for load in loads:
        load.start()
    for load in loads:
        load.wait()
    chans, width = white_ref.shape[1:]
    spectra = jnp.dot(raw_ref[0], basis_ref[...], preferred_element_type=jnp.float32)
    power = jnp.mean(spectra * spectra, axis=-1, keepdims=True) + 1e-06
    mask = jnp.transpose(jnp.broadcast_to(valid_ref[...].astype(jnp.float32), (width, chans)))
    white = (spectra * lax.rsqrt(power) * mask).astype(jnp.bfloat16)
    white_ref[0] = white
    for peer in range(send_ref.shape[0]):
        send_ref[peer] = white


def whiten(raw, valid, basis, out):
    anywhere = pl.BlockSpec(memory_space=pl.ANY)
    return pl.pallas_call(
        whiten_kernel,
        in_specs=[anywhere] * 3,
        out_specs=jax.tree.map(lambda _: VMEM_SPEC, out),
        out_shape=out,
        scratch_shapes=[
            pltpu.VMEM(raw.shape, raw.dtype),
            pltpu.VMEM(valid.shape, valid.dtype),
            pltpu.VMEM(basis.shape, basis.dtype),
            pltpu.SemaphoreType.DMA((3,)),
        ],
        name="whiten",
    )(raw, valid, basis)


def spread_kernel(block_ref, send_ref):
    for peer in range(send_ref.shape[0]):
        send_ref[peer] = block_ref[0]


def rotate_kernel(slot_ref, own_ref, table_ref, mod_ref):
    windows, chans, width = own_ref.shape
    lags = mod_ref.shape[0] // chans
    for lag in range(lags):
        turn = table_ref[pl.ds(slot_ref[0] * lags + lag, 1), :]
        cos, sin = turn[:, :width], turn[:, width:]
        for w in range(windows):
            own = own_ref[w].astype(jnp.float32)
            turned = own * cos + pltpu.roll(own, width // 2, 1) * sin
            mod_ref[lag * chans : (lag + 1) * chans, w * width : (w + 1) * width] = turned.astype(
                jnp.bfloat16
            )


def choose_kernel(odd_ref, own_ref, far_ref, out_ref):
    @pl.when(odd_ref[0] == 1)
    def _():
        out_ref[...] = own_ref[...]

    @pl.when(odd_ref[0] == 0)
    def _():
        out_ref[...] = far_ref[...]


def corr_kernel(mod_ref, other_ref, out_ref, *, scale):
    windows, chans, _ = other_ref.shape
    rows = pl.multiple_of(pl.program_id(0) * chans, chans)
    other = jnp.concatenate([other_ref[w] for w in range(windows)], axis=1)
    total = lax.dot_general(
        mod_ref[pl.ds(rows, chans), :],
        other,
        (((1,), (1,)), ((), ())),
        preferred_element_type=jnp.float32,
    )
    out_ref[...] = total * scale


def correlate(mod, other, lags, scale, name):
    chans = other.shape[1]
    return pl.pallas_call(
        functools.partial(corr_kernel, scale=scale),
        grid=(lags,),
        in_specs=[VMEM_SPEC, VMEM_SPEC],
        out_specs=pl.BlockSpec((chans, chans), lambda lag: (0, lag)),
        out_shape=jax.ShapeDtypeStruct((chans, lags * chans), jnp.float32),
        name=name,
    )(in_vmem(mod), in_vmem(other))


def local(raw, valid):
    windows, chans, samples = raw.shape
    freqs = samples // 2
    groups = lax.axis_size("tm")
    pairs = lax.axis_size("pair")
    total = windows * groups
    lags = LAGS // groups
    scale = 1.0 / math.sqrt(total * freqs)
    slot = lax.axis_index("tm")
    odd = lax.axis_index("pair") & 1
    basis = jnp.asarray(make_basis(samples, freqs))
    table = jnp.asarray(lag_tables(LAGS, freqs, samples))
    spread = pltpu.VMEM((total, chans, samples), jnp.bfloat16)
    white, own_sends = whiten(
        raw, valid, basis, (pltpu.VMEM((windows, chans, samples), jnp.bfloat16), spread)
    )
    own = lax.all_to_all(own_sends, "tm", 0, 0, tiled=True)
    far_white = lax.ppermute(white, "pair", [(p, (p - 2) % pairs) for p in range(pairs)])
    far_sends = on_chip(spread_kernel, "spread", spread, far_white)
    far = lax.all_to_all(far_sends, "tm", 0, 0, tiled=True)
    mod = on_chip(
        rotate_kernel,
        "rotate",
        pltpu.VMEM((lags * chans, total * samples), jnp.bfloat16),
        own,
        table,
        scalars=(slot,),
    )
    swap = on_chip(choose_kernel, "choose", spread, own, far, scalars=(odd,))
    swap, mod = lax.optimization_barrier((swap, mod))
    near = lax.ppermute(swap, "pair", [(p, p ^ 1) for p in range(pairs)])
    far_corr = correlate(mod, far, lags, scale, "far_corr")
    near_corr = correlate(mod, near, lags, scale, "near_corr")
    return (near_corr, far_corr)


def solution(mesh):
    return jax.shard_map(
        local,
        mesh=mesh,
        in_specs=(P("tm", "pair", None), P("tm", "pair")),
        out_specs=(P("pair", "tm"), P("pair", "tm")),
        check_vma=False,
    )
```

time: 154 us -> 45.8 us (0.30)
  waiting for transfers between devices: 111 us -> 8.55 us
  between operations: 14.2 us -> 0.68 us
  starting transfers between devices: 17.3 us -> 30 us
  Pallas kernels: 0 us -> 6.18 us
  other arithmetic: 5.49 us -> 0 us
  matrix products: 4.32 us -> 0 us
    reduce_scatter x2 -> x0, waiting for transfers between devices: 109 us -> none  [the longest x1 58.2 us: local(): lax.psum_scatter(near_part.astype(jnp.float32).astype(jnp.bfloat16), 'tm'...]
    all_to_all x0 -> x2, starting transfers between devices: none -> 11.9 us  [the longest x1 6.66 us: local(): own = lax.all_to_all(own_sends, 'tm', 0, 0, tiled=True)]
    all_to_all x0 -> x2, waiting for transfers between devices: none -> 7.13 us  [the longest x1 7.13 us: local(): far = lax.all_to_all(far_sends, 'tm', 0, 0, tiled=True)]
    pallas_call x0 -> x6, Pallas kernels: none -> 6.18 us  [the longest x2 2.79 us: correlate(): pl.pallas_call(functools.partial(corr_kernel, scale=scale), grid=(lags,),...]
    convert_element_type x5 -> x0, other arithmetic: 4.43 us -> none  [the longest x1 1.8 us: local(): far_corr = lax.psum_scatter(far_part.astype(jnp.float32).astype(jnp.bfloa...]
    dot_general x3 -> x0, matrix products: 4.32 us -> none  [the longest x2 4.13 us: correlate(): total = jnp.dot(left, modded, preferred_element_type=jnp.float32)]
  transfers between devices with their start and end apart: 4 -> 4, of which waited for: 3 -> 3; matrix products, arithmetic and copies ran while one was open for 3% -> 0% of each run, Pallas kernels for 0% -> 6%
where the time goes in v2:
time: 45.8 us; the launch traced here: 45.4 us
  starting transfers between devices  30 us (66%)
  waiting for transfers between devices  8.55 us (19%)
  Pallas kernels  6.18 us (13%)
  between operations  0.68 us (1%)
    ppermute x1, starting transfers between devices, local(): lax.ppermute(white, 'pair', [(p, (p - 2) % pairs) for p in range(pairs)])  12.6 us
    all_to_all x1, waiting for transfers between devices, local(): far = lax.all_to_all(far_sends, 'tm', 0, 0, tiled=True)  7.13 us
    all_to_all x1, starting transfers between devices, local(): own = lax.all_to_all(own_sends, 'tm', 0, 0, tiled=True)  6.66 us
    ppermute x1, starting transfers between devices, local(): near = lax.ppermute(swap, 'pair', [(p, p ^ 1) for p in range(pairs)])  5.41 us
    all_to_all x1, starting transfers between devices, local(): far = lax.all_to_all(far_sends, 'tm', 0, 0, tiled=True)  5.28 us
    pallas_call x2, Pallas kernels, correlate(): pl.pallas_call(functools.partial(corr_kernel, scale=scale), grid=(lags,),...  2.79 us
    pallas_call x1, Pallas kernels, whiten(): pl.pallas_call(whiten_kernel, in_specs=[anywhere] * 3, out_specs=jax.tree...  1.99 us
    pallas_call x3, Pallas kernels, on_chip(): pl.pallas_call(kernel, in_specs=[pl.BlockSpec(memory_space=pltpu.SMEM)] *...  1.4 us
  transfers between devices with their start and end apart: 4, of which 3 were waited for; matrix products, arithmetic and copies ran while one was open for 0% of the time, Pallas kernels for 6%

profile of v2, /device:TPU:1, one launch (start us, length us, event | category | flops | bytes accessed | tf_op | source)
XLA Modules:
  0.0 45.4 jit_solution(13412816249848624426)
XLA Ops:
  0.6 2.0 %whiten.1 = (bf16[1,256,128]{2,1,0:T(8,128)(2,1)S(1)}, bf16[8,256,128]{2,1,0:T(8,128)(2,1)}) custom-call(bf16[1,256,128]{2,1,0:T(8,128)(2,1)} %raw_hbm.1, s32[1,256]{1,0:T(1,128)} %valid_hbm.1, bf16[128,128]{1,0:T(8,128)(2,1)} %constant.15.clone.basis_hbm), custom_call_target="tpu_custom_call" | custom-call | tf_op jit(solution)/shard_map/whiten/pallas_call | solution.py:70
  2.6 6.7 %all-to-all-start = ((bf16[8,256,128]{2,1,0:T(8,128)(2,1)}), bf16[8,256,128]{2,1,0:T(8,128)(2,1)S(1)}, u32[]{:S(2)}, u32[]{:S(2)}) async-start(bf16[8,256,128]{2,1,0:T(8,128)(2,1)} %get-tuple-element.6), calls=%async_computation | async-start | bytes 1048576 | tf_op jit(solution)/shard_map/all_to_all | solution.py:155
  9.3 12.6 %collective-permute-start = (bf16[1,256,128]{2,1,0:T(8,128)(2,1)S(1)}, bf16[1,256,128]{2,1,0:T(8,128)(2,1)S(1)}, u32[]{:S(2)}, u32[]{:S(2)}) collective-permute-start(bf16[1,256,128]{2,1,0:T(8,128)(2,1)S(1)} %get-tuple-element.7), channel_id=1, source_target_pairs={{0,496},{8,504},{16,0},{24,8},{32,16},{40,24},{48,32},{56,40},{64,... | collective-permute-start | bytes 196616 | tf_op jit(solution)/shard_map/ppermute | solution.py:156
  21.9 1.3 %collective-permute-done.block_ref = bf16[1,256,128]{2,1,0:T(8,128)(2,1)S(1)} collective-permute-done((bf16[1,256,128]{2,1,0:T(8,128)(2,1)S(1)}, bf16[1,256,128]{2,1,0:T(8,128)(2,1)S(1)}, u32[]{:S(2)}, u32[]{:S(2)}) %collective-permute-start) | collective-permute-done | bytes 65568 | tf_op jit(solution)/shard_map/ppermute | solution.py:156
  23.3 0.9 %spread.1 = bf16[8,256,128]{2,1,0:T(8,128)(2,1)} custom-call(bf16[1,256,128]{2,1,0:T(8,128)(2,1)S(1)} %collective-permute-done.block_ref), custom_call_target="tpu_custom_call" | custom-call | tf_op jit(solution)/shard_map/spread/pallas_call | solution.py:42
  24.1 0.0 all-to-all-done.own_ref
  24.1 0.0 copy-start
  24.1 5.3 %all-to-all-start.1 = ((bf16[8,256,128]{2,1,0:T(8,128)(2,1)}), bf16[8,256,128]{2,1,0:T(8,128)(2,1)S(1)}, u32[]{:S(2)}, u32[]{:S(2)}) async-start(bf16[8,256,128]{2,1,0:T(8,128)(2,1)} %spread.1), calls=%async_computation.1 | async-start | bytes 1048576 | tf_op jit(solution)/shard_map/all_to_all | solution.py:158
  29.4 0.0 copy-done
  29.4 0.5 %rotate.1.mod_ref = bf16[512,1024]{1,0:T(8,128)(2,1)S(1)} custom-call(s32[1]{0:T(128)} %bitcast.1.slot_ref, bf16[8,256,128]{2,1,0:T(8,128)(2,1)S(1)} %all-to-all-done.own_ref, f32[16,256]{1,0:T(8,128)S(1)} %copy-done), custom_call_target="tpu_custom_call" | custom-call | tf_op jit(solution)/shard_map/rotate/pallas_call | solution.py:42
  29.9 7.1 %all-to-all-done.1.far_ref.other_ref = bf16[8,256,128]{2,1,0:T(8,128)(2,1)S(1)} async-done(((bf16[8,256,128]{2,1,0:T(8,128)(2,1)}), bf16[8,256,128]{2,1,0:T(8,128)(2,1)S(1)}, u32[]{:S(2)}, u32[]{:S(2)}) %all-to-all-start.1) | async-done | bytes 524320 | tf_op jit(solution)/shard_map/all_to_all | solution.py:158
  37.1 5.4 %collective-permute-start.1 = (bf16[8,256,128]{2,1,0:T(8,128)(2,1)S(1)}, bf16[8,256,128]{2,1,0:T(8,128)(2,1)S(1)}, u32[]{:S(2)}, u32[]{:S(2)}) collective-permute-start(bf16[8,256,128]{2,1,0:T(8,128)(2,1)S(1)} %choose.1), channel_id=1, source_target_pairs={{0,8},{8,0},{16,24},{24,16},{32,40},{40,32},{48,56},{56,48},{64,72... | collective-permute-start | bytes 1572872 | tf_op jit(solution)/shard_map/ppermute | solution.py:169
  42.5 1.4 %far_corr.1 = f32[256,512]{1,0:T(8,128)} custom-call(bf16[512,1024]{1,0:T(8,128)(2,1)S(1)} %rotate.1.mod_ref, bf16[8,256,128]{2,1,0:T(8,128)(2,1)S(1)} %all-to-all-done.1.far_ref.other_ref), custom_call_target="tpu_custom_call" | custom-call | tf_op jit(solution)/shard_map/far_corr/pallas_call | solution.py:129
  43.9 0.1 collective-permute-done.1.other_ref
  44.0 1.4 %near_corr.1 = f32[256,512]{1,0:T(8,128)} custom-call(bf16[512,1024]{1,0:T(8,128)(2,1)S(1)} %rotate.1.mod_ref, bf16[8,256,128]{2,1,0:T(8,128)(2,1)S(1)} %collective-permute-done.1.other_ref), custom_call_target="tpu_custom_call" | custom-call | tf_op jit(solution)/shard_map/near_corr/pallas_call | solution.py:129
  (1 shorter events, 0.0 us)
Async XLA Ops:
  2.6 21.5 %all-to-all-start = ((bf16[8,256,128]{2,1,0:T(8,128)(2,1)}), bf16[8,256,128]{2,1,0:T(8,128)(2,1)S(1)}, u32[]{:S(2)}, u32[]{:S(2)}) async-start(bf16[8,256,128]{2,1,0:T(8,128)(2,1)} %get-tuple-element.6), calls=%async_computation | async-start | bytes 1048576 | tf_op jit(solution)/shard_map/all_to_all | solution.py:155
  9.3 14.0 %collective-permute-start = (bf16[1,256,128]{2,1,0:T(8,128)(2,1)S(1)}, bf16[1,256,128]{2,1,0:T(8,128)(2,1)S(1)}, u32[]{:S(2)}, u32[]{:S(2)}) collective-permute-start(bf16[1,256,128]{2,1,0:T(8,128)(2,1)S(1)} %get-tuple-element.7), channel_id=1, source_target_pairs={{0,496},{8,504},{16,0},{24,8},{32,16},{40,24},{48,32},{56,40},{64,... | collective-permute-start | bytes 196616 | tf_op jit(solution)/shard_map/ppermute | solution.py:156
  24.1 5.3 %copy-start = (f32[16,256]{1,0:T(8,128)S(1)}, f32[16,256]{1,0:T(8,128)}, u32[]{:S(2)}) copy-start(f32[16,256]{1,0:T(8,128)} %constant.16.clone.table_ref) | copy-start | bytes 49156
  24.1 12.9 %all-to-all-start.1 = ((bf16[8,256,128]{2,1,0:T(8,128)(2,1)}), bf16[8,256,128]{2,1,0:T(8,128)(2,1)S(1)}, u32[]{:S(2)}, u32[]{:S(2)}) async-start(bf16[8,256,128]{2,1,0:T(8,128)(2,1)} %spread.1), calls=%async_computation.1 | async-start | bytes 1048576 | tf_op jit(solution)/shard_map/all_to_all | solution.py:158
  37.1 6.9 %collective-permute-start.1 = (bf16[8,256,128]{2,1,0:T(8,128)(2,1)S(1)}, bf16[8,256,128]{2,1,0:T(8,128)(2,1)S(1)}, u32[]{:S(2)}, u32[]{:S(2)}) collective-permute-start(bf16[8,256,128]{2,1,0:T(8,128)(2,1)S(1)} %choose.1), channel_id=1, source_target_pairs={{0,8},{8,0},{16,24},{24,16},{32,40},{40,32},{48,56},{56,48},{64,72... | collective-permute-start | bytes 1572872 | tf_op jit(solution)/shard_map/ppermute | solution.py:169

commit v3 on v2

v3 whole, which is shorter than its diff:
```python
import functools
import math

import jax
import jax.numpy as jnp
import numpy as np
from jax import lax
from jax.experimental import pallas as pl
from jax.experimental.pallas import tpu as pltpu
from jax.sharding import PartitionSpec as P

LAGS = 16


def make_basis(samples, freqs):
    times = np.arange(samples, dtype=np.float64)[:, None]
    bins = np.arange(freqs, dtype=np.float64)[None, :]
    hann = 0.5 - 0.5 * np.cos(2.0 * math.pi * times / samples)
    angle = 2.0 * math.pi * bins * times / samples
    return np.concatenate([hann * np.cos(angle), -hann * np.sin(angle)], axis=1).astype(
        jnp.bfloat16
    )


def lag_tables(lags, freqs, samples):
    shift_lag = np.arange(lags, dtype=np.float64)[:, None] - lags // 2
    bins = np.arange(freqs, dtype=np.float64)[None, :]
    theta = 2.0 * math.pi * bins * shift_lag / samples
    cos = np.cos(theta).astype(jnp.bfloat16).astype(np.float32)
    sin = np.sin(theta).astype(jnp.bfloat16).astype(np.float32)
    return np.concatenate([cos, cos, -sin, sin], axis=1)


def in_vmem(value):
    return pltpu.with_memory_space_constraint(value, pltpu.VMEM)


VMEM_SPEC = pl.BlockSpec(memory_space=pltpu.VMEM)


def on_chip(kernel, name, out, *args):
    return pl.pallas_call(
        kernel,
        in_specs=[VMEM_SPEC] * len(args),
        out_specs=jax.tree.map(lambda _: VMEM_SPEC, out),
        out_shape=out,
        name=name,
    )(*[in_vmem(arg) for arg in args])


def whiten_kernel(raw_hbm, valid_hbm, basis_hbm, white_ref, raw_ref, valid_ref, basis_ref, sems):
    moves = ((raw_hbm, raw_ref), (basis_hbm, basis_ref), (valid_hbm, valid_ref))
    loads = [pltpu.make_async_copy(src, dst, sems.at[i]) for i, (src, dst) in enumerate(moves)]
    for load in loads:
        load.start()
    for load in loads:
        load.wait()
    chans, width = white_ref.shape[1:]
    spectra = jnp.dot(raw_ref[0], basis_ref[...], preferred_element_type=jnp.float32)
    power = jnp.mean(spectra * spectra, axis=-1, keepdims=True) + 1e-06
    mask = jnp.transpose(jnp.broadcast_to(valid_ref[...].astype(jnp.float32), (width, chans)))
    white_ref[0] = (spectra * lax.rsqrt(power) * mask).astype(jnp.bfloat16)


def whiten(raw, valid, basis):
    anywhere = pl.BlockSpec(memory_space=pl.ANY)
    return pl.pallas_call(
        whiten_kernel,
        in_specs=[anywhere] * 3,
        out_specs=VMEM_SPEC,
        out_shape=pltpu.VMEM(raw.shape, jnp.bfloat16),
        scratch_shapes=[
            pltpu.VMEM(raw.shape, raw.dtype),
            pltpu.VMEM(valid.shape, valid.dtype),
            pltpu.VMEM(basis.shape, basis.dtype),
            pltpu.SemaphoreType.DMA((3,)),
        ],
        name="whiten",
    )(raw, valid, basis)


def slots_of(chans):
    odd = lax.axis_index("pair") & 1
    return pl.multiple_of(odd * chans, chans), pl.multiple_of((1 - odd) * chans, chans)


def slots_kernel(white_ref, far_ref, send_ref):
    peers, both, _ = send_ref.shape
    chans = both // 2
    own_at, far_at = slots_of(chans)
    for peer in range(peers):
        send_ref[peer, pl.ds(own_at, chans), :] = white_ref[0]
        send_ref[peer, pl.ds(far_at, chans), :] = far_ref[0]


def far_kernel(gath_ref, table_ref, out_ref, mod_ref, *, scale):
    windows, both, width = gath_ref.shape
    chans = both // 2
    lag = pl.program_id(0)
    own_at, far_at = slots_of(chans)
    rows = pl.multiple_of(lag * chans, chans)
    turn = table_ref[pl.ds(lax.axis_index("tm") * pl.num_programs(0) + lag, 1), :]
    cos, sin = turn[:, :width], turn[:, width:]
    for w in range(windows):
        own = gath_ref[w, pl.ds(own_at, chans), :].astype(jnp.float32)
        turned = own * cos + pltpu.roll(own, width // 2, 1) * sin
        mod_ref[pl.ds(rows, chans), w * width : (w + 1) * width] = turned.astype(jnp.bfloat16)
    other = jnp.concatenate(
        [gath_ref[w, pl.ds(far_at, chans), :] for w in range(windows)], axis=1
    )
    total = lax.dot_general(
        mod_ref[pl.ds(rows, chans), :],
        other,
        (((1,), (1,)), ((), ())),
        preferred_element_type=jnp.float32,
    )
    out_ref[...] = total * scale


def correlate_far(gathered, table, lags, scale):
    windows, both, width = gathered.shape
    chans = both // 2
    return pl.pallas_call(
        functools.partial(far_kernel, scale=scale),
        grid=(lags,),
        in_specs=[VMEM_SPEC, VMEM_SPEC],
        out_specs=[pl.BlockSpec((chans, chans), lambda lag: (0, lag)), VMEM_SPEC],
        out_shape=[
            jax.ShapeDtypeStruct((chans, lags * chans), jnp.float32),
            pltpu.VMEM((lags * chans, windows * width), jnp.bfloat16),
        ],
        name="far_corr",
    )(in_vmem(gathered), in_vmem(table))


def corr_kernel(mod_ref, other_ref, out_ref, *, scale):
    windows, chans, _ = other_ref.shape
    rows = pl.multiple_of(pl.program_id(0) * chans, chans)
    other = jnp.concatenate([other_ref[w] for w in range(windows)], axis=1)
    total = lax.dot_general(
        mod_ref[pl.ds(rows, chans), :],
        other,
        (((1,), (1,)), ((), ())),
        preferred_element_type=jnp.float32,
    )
    out_ref[...] = total * scale


def correlate(mod, other, lags, scale, name):
    chans = other.shape[1]
    return pl.pallas_call(
        functools.partial(corr_kernel, scale=scale),
        grid=(lags,),
        in_specs=[VMEM_SPEC, VMEM_SPEC],
        out_specs=pl.BlockSpec((chans, chans), lambda lag: (0, lag)),
        out_shape=jax.ShapeDtypeStruct((chans, lags * chans), jnp.float32),
        name=name,
    )(in_vmem(mod), in_vmem(other))


def local(raw, valid):
    windows, chans, samples = raw.shape
    freqs = samples // 2
    groups = lax.axis_size("tm")
    pairs = lax.axis_size("pair")
    total = windows * groups
    lags = LAGS // groups
    scale = 1.0 / math.sqrt(total * freqs)
    basis = jnp.asarray(make_basis(samples, freqs))
    table = jnp.asarray(lag_tables(LAGS, freqs, samples))
    white = whiten(raw, valid, basis)
    far = lax.ppermute(white, "pair", [(p, (p - 2) % pairs) for p in range(pairs)])
    sends = on_chip(
        slots_kernel, "slots", pltpu.VMEM((total, 2 * chans, samples), jnp.bfloat16), white, far
    )
    gathered = lax.all_to_all(sends, "tm", 0, 0, tiled=True)
    near = lax.ppermute(gathered[:, chans:, :], "pair", [(p, p ^ 1) for p in range(pairs)])
    far_corr, mod = correlate_far(gathered, table, lags, scale)
    near_corr = correlate(mod, near, lags, scale, "near_corr")
    return (near_corr, far_corr)


def solution(mesh):
    return jax.shard_map(
        local,
        mesh=mesh,
        in_specs=(P("tm", "pair", None), P("tm", "pair")),
        out_specs=(P("pair", "tm"), P("pair", "tm")),
        check_vma=False,
    )
```

time: 45.8 us -> 44.3 us (0.967)
  blocking collectives: 0 us -> 18.7 us
  starting transfers between devices: 30 us -> 19 us
  waiting for transfers between devices: 8.55 us -> 1.31 us
  Pallas kernels: 6.18 us -> 4.38 us
    all_to_all x0 -> x1, blocking collectives: none -> 18.7 us  [local(): gathered = lax.all_to_all(sends, 'tm', 0, 0, tiled=True)]
    all_to_all x2 -> x0, starting transfers between devices: 11.9 us -> none  [the longest x1 6.66 us: local(): own = lax.all_to_all(own_sends, 'tm', 0, 0, tiled=True)]
    all_to_all x2 -> x0, waiting for transfers between devices: 7.13 us -> none  [the longest x1 7.13 us: local(): far = lax.all_to_all(far_sends, 'tm', 0, 0, tiled=True)]
    ppermute x1, starting transfers between devices: 12.6 us -> 14.4 us  [local(): lax.ppermute(white, 'pair', [(p, (p - 2) % pairs) for p in range(pairs)])]
    pallas_call x2 -> x1, Pallas kernels: 2.79 us -> 1.38 us  [correlate(): pl.pallas_call(functools.partial(corr_kernel, scale=scale), grid=(lags,),...]
    ppermute x1, starting transfers between devices: 5.41 us -> 4.57 us  [local(): lax.ppermute(gathered[:, chans:, :], 'pair', [(p, p ^ 1) for p in range(p...]
    pallas_call x4 -> x3, Pallas kernels: 3.39 us -> 2.99 us  [the longest x1 1.67 us: correlate_far(): pl.pallas_call(functools.partial(far_kernel, scale=scale), grid=(lags,),...]
  transfers between devices with their start and end apart: 4 -> 2, of which waited for: 3 -> 1; matrix products, arithmetic and copies ran while one was open for 0% -> 0% of each run, Pallas kernels for 6% -> 4%
where the time goes in v3:
time: 44.3 us; the launch traced here: 44.1 us
  starting transfers between devices  19 us (43%)
  blocking collectives  18.7 us (42%)
  Pallas kernels  4.38 us (10%)
  waiting for transfers between devices  1.31 us (3%)
  between operations  0.67 us (2%)
    all_to_all x1, blocking collectives, local(): gathered = lax.all_to_all(sends, 'tm', 0, 0, tiled=True)  18.7 us
    ppermute x1, starting transfers between devices, local(): lax.ppermute(white, 'pair', [(p, (p - 2) % pairs) for p in range(pairs)])  14.4 us
    ppermute x1, starting transfers between devices, local(): lax.ppermute(gathered[:, chans:, :], 'pair', [(p, p ^ 1) for p in range(p...  4.57 us
    pallas_call x1, Pallas kernels, correlate_far(): pl.pallas_call(functools.partial(far_kernel, scale=scale), grid=(lags,),...  1.67 us
    pallas_call x1, Pallas kernels, correlate(): pl.pallas_call(functools.partial(corr_kernel, scale=scale), grid=(lags,),...  1.38 us
    ppermute x1, waiting for transfers between devices, local(): lax.ppermute(white, 'pair', [(p, (p - 2) % pairs) for p in range(pairs)])  1.31 us
    pallas_call x1, Pallas kernels, whiten(): pl.pallas_call(whiten_kernel, in_specs=[anywhere] * 3, out_specs=VMEM_SPE...  1.17 us
  transfers between devices with their start and end apart: 2, of which 1 were waited for; matrix products, arithmetic and copies ran while one was open for 0% of the time, Pallas kernels for 4%

profile of v3, /device:TPU:1, one launch (start us, length us, event | category | flops | bytes accessed | tf_op | source)
XLA Modules:
  0.0 44.1 jit_solution(7942281515576955182)
XLA Ops:
  0.6 1.2 %whiten.1.white_ref = bf16[1,256,128]{2,1,0:T(8,128)(2,1)S(1)} custom-call(bf16[1,256,128]{2,1,0:T(8,128)(2,1)} %raw_hbm.1, s32[1,256]{1,0:T(1,128)} %valid_hbm.1, bf16[128,128]{1,0:T(8,128)(2,1)} %constant.4.clone.basis_hbm), custom_call_target="tpu_custom_call" | custom-call | tf_op jit(solution)/shard_map/whiten/pallas_call | solution.py:67
  1.8 14.4 %collective-permute-start = (bf16[1,256,128]{2,1,0:T(8,128)(2,1)S(1)}, bf16[1,256,128]{2,1,0:T(8,128)(2,1)S(1)}, u32[]{:S(2)}, u32[]{:S(2)}) collective-permute-start(bf16[1,256,128]{2,1,0:T(8,128)(2,1)S(1)} %whiten.1.white_ref), channel_id=1, source_target_pairs={{0,496},{8,504},{16,0},{24,8},{32,16},{40,24},{48,32},{56,40},{64,... | collective-permute-start | bytes 196616 | tf_op jit(solution)/shard_map/ppermute | solution.py:172
  16.2 1.3 %collective-permute-done.far_ref = bf16[1,256,128]{2,1,0:T(8,128)(2,1)S(1)} collective-permute-done((bf16[1,256,128]{2,1,0:T(8,128)(2,1)S(1)}, bf16[1,256,128]{2,1,0:T(8,128)(2,1)S(1)}, u32[]{:S(2)}, u32[]{:S(2)}) %collective-permute-start) | collective-permute-done | bytes 65568 | tf_op jit(solution)/shard_map/ppermute | solution.py:172
  17.5 0.1 slots.1
  17.7 18.7 %all_to_all.5.gath_ref = bf16[8,512,128]{2,1,0:T(8,128)(2,1)S(1)} all-to-all(bf16[8,512,128]{2,1,0:T(8,128)(2,1)S(1)} %slots.1), channel_id=1, replica_groups=mesh['pair'=64,'tm'=8] {'tm'}, dimensions={0} | all-to-all | bytes 2097152 | tf_op jit(solution)/shard_map/all_to_all | solution.py:176
  36.4 0.0 copy-start
  36.4 4.6 %collective-permute-start.1 = (bf16[8,256,128]{2,1,0:T(8,128)(2,1)S(1)}, bf16[8,256,128]{2,1,0:T(8,128)(2,1)S(1)}, u32[]{:S(2)}, u32[]{:S(2)}) collective-permute-start(bf16[8,256,128]{2,1,0:T(8,128)(2,1)S(1)} %slice.4), channel_id=1, source_target_pairs={{0,8},{8,0},{16,24},{24,16},{32,40},{40,32},{48,56},{56,48},{64,72... | collective-permute-start | bytes 1572872 | tf_op jit(solution)/shard_map/ppermute | solution.py:177
  41.0 0.0 copy-done
  41.0 1.7 %far_corr.1 = (f32[256,512]{1,0:T(8,128)}, bf16[512,1024]{1,0:T(8,128)(2,1)S(1)}) custom-call(bf16[8,512,128]{2,1,0:T(8,128)(2,1)S(1)} %all_to_all.5.gath_ref, f32[16,256]{1,0:T(8,128)S(1)} %copy-done), custom_call_target="tpu_custom_call" | custom-call | tf_op jit(solution)/shard_map/far_corr/pallas_call | solution.py:123
  42.7 0.0 collective-permute-done.1.other_ref
  42.7 1.4 %near_corr.1 = f32[256,512]{1,0:T(8,128)} custom-call(bf16[512,1024]{1,0:T(8,128)(2,1)S(1)} %get-tuple-element.4.mod_ref, bf16[8,256,128]{2,1,0:T(8,128)(2,1)S(1)} %collective-permute-done.1.other_ref), custom_call_target="tpu_custom_call" | custom-call | tf_op jit(solution)/shard_map/near_corr/pallas_call | solution.py:151
  (1 shorter events, 0.0 us)
Async XLA Ops:
  1.8 15.7 %collective-permute-start = (bf16[1,256,128]{2,1,0:T(8,128)(2,1)S(1)}, bf16[1,256,128]{2,1,0:T(8,128)(2,1)S(1)}, u32[]{:S(2)}, u32[]{:S(2)}) collective-permute-start(bf16[1,256,128]{2,1,0:T(8,128)(2,1)S(1)} %whiten.1.white_ref), channel_id=1, source_target_pairs={{0,496},{8,504},{16,0},{24,8},{32,16},{40,24},{48,32},{56,40},{64,... | collective-permute-start | bytes 196616 | tf_op jit(solution)/shard_map/ppermute | solution.py:172
  36.4 4.6 %copy-start = (f32[16,256]{1,0:T(8,128)S(1)}, f32[16,256]{1,0:T(8,128)}, u32[]{:S(2)}) copy-start(f32[16,256]{1,0:T(8,128)} %constant.5.clone.table_ref) | copy-start | bytes 49156
  36.4 6.3 %collective-permute-start.1 = (bf16[8,256,128]{2,1,0:T(8,128)(2,1)S(1)}, bf16[8,256,128]{2,1,0:T(8,128)(2,1)S(1)}, u32[]{:S(2)}, u32[]{:S(2)}) collective-permute-start(bf16[8,256,128]{2,1,0:T(8,128)(2,1)S(1)} %slice.4), channel_id=1, source_target_pairs={{0,8},{8,0},{16,24},{24,16},{32,40},{40,32},{48,56},{56,48},{64,72... | collective-permute-start | bytes 1572872 | tf_op jit(solution)/shard_map/ppermute | solution.py:177

commit v4 on v3

--- a/solution.py
+++ b/solution.py
@@ -48,27 +48,30 @@
     )(*[in_vmem(arg) for arg in args])
 
 
-def whiten_kernel(raw_hbm, valid_hbm, basis_hbm, white_ref, raw_ref, valid_ref, basis_ref, sems):
+def whiten_kernel(raw_hbm, valid_hbm, basis_hbm, *refs):
+    *white_refs, raw_ref, valid_ref, basis_ref, sems = refs
     moves = ((raw_hbm, raw_ref), (basis_hbm, basis_ref), (valid_hbm, valid_ref))
     loads = [pltpu.make_async_copy(src, dst, sems.at[i]) for i, (src, dst) in enumerate(moves)]
     for load in loads:
         load.start()
     for load in loads:
         load.wait()
-    chans, width = white_ref.shape[1:]
+    chans, width = white_refs[0].shape[1:]
     spectra = jnp.dot(raw_ref[0], basis_ref[...], preferred_element_type=jnp.float32)
     power = jnp.mean(spectra * spectra, axis=-1, keepdims=True) + 1e-06
     mask = jnp.transpose(jnp.broadcast_to(valid_ref[...].astype(jnp.float32), (width, chans)))
-    white_ref[0] = (spectra * lax.rsqrt(power) * mask).astype(jnp.bfloat16)
-
-
-def whiten(raw, valid, basis):
+    white = (spectra * lax.rsqrt(power) * mask).astype(jnp.bfloat16)
+    for white_ref in white_refs:
+        white_ref[0] = white
+
+
+def whiten(raw, valid, basis, copies):
     anywhere = pl.BlockSpec(memory_space=pl.ANY)
     return pl.pallas_call(
         whiten_kernel,
         in_specs=[anywhere] * 3,
-        out_specs=VMEM_SPEC,
-        out_shape=pltpu.VMEM(raw.shape, jnp.bfloat16),
+        out_specs=[VMEM_SPEC] * copies,
+        out_shape=[pltpu.VMEM(raw.shape, jnp.bfloat16)] * copies,
         scratch_shapes=[
             pltpu.VMEM(raw.shape, raw.dtype),
             pltpu.VMEM(valid.shape, valid.dtype),
@@ -91,6 +94,43 @@
     for peer in range(peers):
         send_ref[peer, pl.ds(own_at, chans), :] = white_ref[0]
         send_ref[peer, pl.ds(far_at, chans), :] = far_ref[0]
+
+
+def spread_kernel(block_ref, send_ref):
+    for peer in range(send_ref.shape[0]):
+        send_ref[peer] = block_ref[0]
+
+
+def merge_kernel(far_ref, early_ref, gath_ref):
+    chans = far_ref.shape[1]
+    own_at, far_at = slots_of(chans)
+    for w in range(far_ref.shape[0]):
+        gath_ref[w, pl.ds(own_at, chans), :] = early_ref[w]
+        gath_ref[w, pl.ds(far_at, chans), :] = far_ref[w]
+
+
+def place_kernel(own_ref, gath_ref):
+    chans = own_ref.shape[1]
+    own_at, _ = slots_of(chans)
+    for w in range(own_ref.shape[0]):
+        gath_ref[w, pl.ds(own_at, chans), :] = own_ref[w]
+
+
+def put_far_kernel(far_ref, old_ref, gath_ref):
+    del old_ref
+    chans = far_ref.shape[1]
+    _, far_at = slots_of(chans)
+    for w in range(far_ref.shape[0]):
+        gath_ref[w, pl.ds(far_at, chans), :] = far_ref[w]
+
+
+def unwritten(shape, dtype):
+    return pl.pallas_call(
+        lambda out_ref: None,
+        out_specs=pl.BlockSpec(memory_space=pl.ANY),
+        out_shape=jax.ShapeDtypeStruct(shape, dtype),
+        name="unwritten",
+    )()
 
 
 def far_kernel(gath_ref, table_ref, out_ref, mod_ref, *, scale):
@@ -158,6 +198,59 @@
     )(in_vmem(mod), in_vmem(other))
 
 
+def gather_windows(whites, pairs, groups):
+    white, for_start, for_both, for_end = whites
+    windows, chans, width = white.shape
+    total = windows * groups
+    at_start = lax.axis_index("pair") < 2
+    at_end = lax.axis_index("pair") >= pairs - 2
+    single = pltpu.VMEM((total, chans, width), white.dtype)
+    double = pltpu.VMEM((total, 2 * chans, width), white.dtype)
+
+    def exchange(sends):
+        return lax.all_to_all(sends, "tm", 0, 0, tiled=True)
+
+    def one(block):
+        return exchange(on_chip(spread_kernel, "spread", single, block))
+
+    def both(white, far):
+        return exchange(on_chip(slots_kernel, "slots", double, white, far))
+
+    def after_own(far, own):
+        return on_chip(merge_kernel, "merge", double, one(far), own)
+
+    def own_alone(white):
+        return on_chip(place_kernel, "place_own", double, one(white))
+
+    def add_far(wrapped, gathered):
+        return pl.pallas_call(
+            put_far_kernel,
+            in_specs=[VMEM_SPEC] * 2,
+            out_specs=VMEM_SPEC,
+            out_shape=double,
+            input_output_aliases={1: 0},
+            name="put_far",
+        )(in_vmem(one(wrapped)), in_vmem(gathered))
+
+    far = lax.ppermute(white, "pair", [(p, p - 2) for p in range(2, pairs)])
+    own = lax.cond(at_start, one, lambda white: unwritten(single.shape, single.dtype), for_start)
+    white, own = lax.optimization_barrier((white, own))
+    wrapped = lax.ppermute(white, "pair", [(0, pairs - 2), (1, pairs - 1)])
+    gathered = lax.switch(
+        at_start.astype(jnp.int32) + 2 * at_end.astype(jnp.int32),
+        (
+            lambda for_both, for_end, far, own: both(for_both, far),
+            lambda for_both, for_end, far, own: after_own(far, own),
+            lambda for_both, for_end, far, own: own_alone(for_end),
+        ),
+        for_both,
+        for_end,
+        far,
+        own,
+    )
+    return lax.cond(at_end, add_far, lambda wrapped, gathered: gathered, wrapped, gathered)
+
+
 def local(raw, valid):
     windows, chans, samples = raw.shape
     freqs = samples // 2
@@ -168,12 +261,8 @@
     scale = 1.0 / math.sqrt(total * freqs)
     basis = jnp.asarray(make_basis(samples, freqs))
     table = jnp.asarray(lag_tables(LAGS, freqs, samples))
-    white = whiten(raw, valid, basis)
-    far = lax.ppermute(white, "pair", [(p, (p - 2) % pairs) for p in range(pairs)])
-    sends = on_chip(
-        slots_kernel, "slots", pltpu.VMEM((total, 2 * chans, samples), jnp.bfloat16), white, far
-    )
-    gathered = lax.all_to_all(sends, "tm", 0, 0, tiled=True)
+    whites = whiten(raw, valid, basis, 4)
+    gathered = gather_windows(whites, pairs, groups)
     near = lax.ppermute(gathered[:, chans:, :], "pair", [(p, p ^ 1) for p in range(pairs)])
     far_corr, mod = correlate_far(gathered, table, lags, scale)
     near_corr = correlate(mod, near, lags, scale, "near_corr")

time: 44.3 us -> 40.6 us (0.916)
  starting transfers between devices: 19 us -> 7.58 us
  blocking collectives: 18.7 us -> 27.4 us
  waiting for transfers between devices: 1.31 us -> 0.01 us
    ppermute x1 -> x2, starting transfers between devices: 14.4 us -> 3.3 us  [the longest x1 2.01 us: gather_windows(): wrapped = lax.ppermute(white, 'pair', [(0, pairs - 2), (1, pairs - 1)])]
    all_to_all x1 -> x2, blocking collectives: 18.7 us -> 27.4 us  [exchange(): return lax.all_to_all(sends, 'tm', 0, 0, tiled=True)]
    ppermute x1 -> x2, waiting for transfers between devices: 1.31 us -> 0.01 us  [the longest x1 0.01 us: gather_windows(): far = lax.ppermute(white, 'pair', [(p, p - 2) for p in range(2, pairs)])]
  transfers between devices with their start and end apart: 2 -> 3, of which waited for: 1 -> 0; matrix products, arithmetic and copies ran while one was open for 0% -> 0% of each run, Pallas kernels for 4% -> 5%
where the time goes in v4:
time: 40.6 us; the launch traced here: 40.3 us
  blocking collectives  27.4 us (67%)
  starting transfers between devices  7.58 us (19%)
  Pallas kernels  4.45 us (11%)
  between operations  0.74 us (2%)
    all_to_all x2, blocking collectives, exchange(): return lax.all_to_all(sends, 'tm', 0, 0, tiled=True)  27.4 us
    ppermute x1, starting transfers between devices, local(): lax.ppermute(gathered[:, chans:, :], 'pair', [(p, p ^ 1) for p in range(p...  4.28 us
    ppermute x1, starting transfers between devices, gather_windows(): wrapped = lax.ppermute(white, 'pair', [(0, pairs - 2), (1, pairs - 1)])  2.01 us
    pallas_call x1, Pallas kernels, correlate_far(): pl.pallas_call(functools.partial(far_kernel, scale=scale), grid=(lags,),...  1.67 us
    pallas_call x1, Pallas kernels, correlate(): pl.pallas_call(functools.partial(corr_kernel, scale=scale), grid=(lags,),...  1.39 us
    ppermute x1, starting transfers between devices, gather_windows(): far = lax.ppermute(white, 'pair', [(p, p - 2) for p in range(2, pairs)])  1.29 us
    pallas_call x1, Pallas kernels, whiten(): pl.pallas_call(whiten_kernel, in_specs=[anywhere] * 3, out_specs=[VMEM_SP...  1.17 us
  transfers between devices with their start and end apart: 3, of which 0 were waited for; matrix products, arithmetic and copies ran while one was open for 0% of the time, Pallas kernels for 5%

profile of v4, /device:TPU:1, one launch (start us, length us, event | category | flops | bytes accessed | tf_op | source)
XLA Modules:
  0.0 40.3 jit_solution(8614098872524796572)
XLA Ops:
  0.6 1.2 %whiten.1 = (bf16[1,256,128]{2,1,0:T(8,128)(2,1)S(1)}, bf16[1,256,128]{2,1,0:T(8,128)(2,1)S(1)}, bf16[1,256,128]{2,1,0:T(8,128)(2,1)S(1)}, bf16[1,256,128]{2,1,0:T(8,128)(2,1)S(1)}) custom-call(bf16[1,256,128]{2,1,0:T(8,128)(2,1)} %raw_hbm.1, s32[1,256]{1,0:T(1,128)} %valid_hbm.1, bf16[128,128]{1,0:T(8,128)(2,1)} %constant.17.clone.basis_hbm), custom_call_target="tpu_custom_call" | custom-call | tf_op jit(solution)/shard_map/whiten/pallas_call | solution.py:70
  1.8 1.3 %collective-permute-start = (bf16[1,256,128]{2,1,0:T(8,128)(2,1)S(1)}, bf16[1,256,128]{2,1,0:T(8,128)(2,1)S(1)}, u32[]{:S(2)}, u32[]{:S(2)}) collective-permute-start(bf16[1,256,128]{2,1,0:T(8,128)(2,1)S(1)} %get-tuple-element.46), channel_id=1, source_target_pairs={{16,0},{24,8},{32,16},{40,24},{48,32},{56,40},{64,48},{72,56},{80,... | collective-permute-start | bytes 196616 | tf_op jit(solution)/shard_map/ppermute | solution.py:235
  3.1 14.1 %conditional.3 = (bf16[8,256,128]{2,1,0:T(8,128)(2,1)S(1)}) conditional(s32[]{:T(128)} %convert_element_type.9, () %tuple.31, bf16[1,256,128]{2,1,0:T(8,128)(2,1)S(1)} %get-tuple-element.43), branch_computations={%region_0.0_spmd, %region_1.0_spmd} | conditional | bytes 1048584 | solution.py:236
  3.1 0.1 spread.4
  3.2 14.0 %all_to_all.20 = bf16[8,256,128]{2,1,0:T(8,128)(2,1)S(1)} all-to-all(bf16[8,256,128]{2,1,0:T(8,128)(2,1)S(1)} %spread.4), channel_id=1, replica_groups=mesh['pair'=64,'tm'=8] {'tm'}, dimensions={0} | all-to-all | bytes 1048576 | tf_op jit(solution)/shard_map/cond/branch_1_fun/all_to_all | solution.py:211
  17.2 2.0 %collective-permute-start.1 = (bf16[1,256,128]{2,1,0:T(8,128)(2,1)S(1)}, bf16[1,256,128]{2,1,0:T(8,128)(2,1)S(1)}, u32[]{:S(2)}, u32[]{:S(2)}) collective-permute-start(bf16[1,256,128]{2,1,0:T(8,128)(2,1)S(1)} %get-tuple-element.46), channel_id=1, source_target_pairs={{0,496},{8,504},{1,497},{9,505},{2,498},{10,506},{3,499},{11,507},... | collective-permute-start | bytes 196616 | tf_op jit(solution)/shard_map/ppermute | solution.py:238
  19.2 0.0 collective-permute-done
  19.2 13.6 %conditional.4 = (bf16[8,512,128]{2,1,0:T(8,128)(2,1)S(1)}) conditional(s32[]{:T(128)} %clamp.3, (bf16[1,256,128]{2,1,0:T(8,128)(2,1)S(1)}, bf16[1,256,128]{2,1,0:T(8,128)(2,1)S(1)}) %tuple.30, (bf16[1,256,128]{2,1,0:T(8,128)(2,1)S(1)}, bf16[8,256,128]{2,1,0:T(8,128)(2,1)S(1)}) %tuple.33, ...), branch_computations={%region_2.0_spmd, %region_3.0_spmd, %region_4.0_spmd} | conditional | bytes 2097160 | solution.py:239
  19.3 0.1 spread.5
  19.3 13.4 %all_to_all.22.far_ref = bf16[8,256,128]{2,1,0:T(8,128)(2,1)S(1)} all-to-all(bf16[8,256,128]{2,1,0:T(8,128)(2,1)S(1)} %spread.5), channel_id=1, replica_groups=mesh['pair'=64,'tm'=8] {'tm'}, dimensions={0} | all-to-all | bytes 1048576 | tf_op jit(solution)/shard_map/cond/branch_1_fun/all_to_all | solution.py:211
  32.7 0.1 merge.1
  32.8 0.0 collective-permute-done.1
  32.9 0.0 copy-start
  32.9 4.3 %collective-permute-start.2 = (bf16[8,256,128]{2,1,0:T(8,128)(2,1)S(1)}, bf16[8,256,128]{2,1,0:T(8,128)(2,1)S(1)}, u32[]{:S(2)}, u32[]{:S(2)}) collective-permute-start(bf16[8,256,128]{2,1,0:T(8,128)(2,1)S(1)} %slice.4), channel_id=1, source_target_pairs={{0,8},{8,0},{16,24},{24,16},{32,40},{40,32},{48,56},{56,48},{64,72... | collective-permute-start | bytes 1572872 | tf_op jit(solution)/shard_map/ppermute | solution.py:266
  37.2 0.0 copy-done
  37.2 1.7 %far_corr.1 = (f32[256,512]{1,0:T(8,128)}, bf16[512,1024]{1,0:T(8,128)(2,1)S(1)}) custom-call(bf16[8,512,128]{2,1,0:T(8,128)(2,1)S(1)} %get-tuple-element.51.gath_ref, f32[16,256]{1,0:T(8,128)S(1)} %copy-done), custom_call_target="tpu_custom_call" | custom-call | tf_op jit(solution)/shard_map/far_corr/pallas_call | solution.py:163
  38.9 0.0 collective-permute-done.2.other_ref
  38.9 1.4 %near_corr.1 = f32[256,512]{1,0:T(8,128)} custom-call(bf16[512,1024]{1,0:T(8,128)(2,1)S(1)} %get-tuple-element.47.mod_ref, bf16[8,256,128]{2,1,0:T(8,128)(2,1)S(1)} %collective-permute-done.2.other_ref), custom_call_target="tpu_custom_call" | custom-call | tf_op jit(solution)/shard_map/near_corr/pallas_call | solution.py:191
  (2 shorter events, 0.0 us)
Async XLA Ops:
  1.8 17.4 %collective-permute-start = (bf16[1,256,128]{2,1,0:T(8,128)(2,1)S(1)}, bf16[1,256,128]{2,1,0:T(8,128)(2,1)S(1)}, u32[]{:S(2)}, u32[]{:S(2)}) collective-permute-start(bf16[1,256,128]{2,1,0:T(8,128)(2,1)S(1)} %get-tuple-element.46), channel_id=1, source_target_pairs={{16,0},{24,8},{32,16},{40,24},{48,32},{56,40},{64,48},{72,56},{80,... | collective-permute-start | bytes 196616 | tf_op jit(solution)/shard_map/ppermute | solution.py:235
  17.2 15.6 %collective-permute-start.1 = (bf16[1,256,128]{2,1,0:T(8,128)(2,1)S(1)}, bf16[1,256,128]{2,1,0:T(8,128)(2,1)S(1)}, u32[]{:S(2)}, u32[]{:S(2)}) collective-permute-start(bf16[1,256,128]{2,1,0:T(8,128)(2,1)S(1)} %get-tuple-element.46), channel_id=1, source_target_pairs={{0,496},{8,504},{1,497},{9,505},{2,498},{10,506},{3,499},{11,507},... | collective-permute-start | bytes 196616 | tf_op jit(solution)/shard_map/ppermute | solution.py:238
  32.9 4.3 %copy-start = (f32[16,256]{1,0:T(8,128)S(1)}, f32[16,256]{1,0:T(8,128)}, u32[]{:S(2)}) copy-start(f32[16,256]{1,0:T(8,128)} %constant.18.clone.table_ref) | copy-start | bytes 49156
  32.9 6.0 %collective-permute-start.2 = (bf16[8,256,128]{2,1,0:T(8,128)(2,1)S(1)}, bf16[8,256,128]{2,1,0:T(8,128)(2,1)S(1)}, u32[]{:S(2)}, u32[]{:S(2)}) collective-permute-start(bf16[8,256,128]{2,1,0:T(8,128)(2,1)S(1)} %slice.4), channel_id=1, source_target_pairs={{0,8},{8,0},{16,24},{24,16},{32,40},{40,32},{48,56},{56,48},{64,72... | collective-permute-start | bytes 1572872 | tf_op jit(solution)/shard_map/ppermute | solution.py:266

commit v5 on v4

--- a/solution.py
+++ b/solution.py
@@ -175,24 +175,21 @@
 
 def corr_kernel(mod_ref, other_ref, out_ref, *, scale):
     windows, chans, _ = other_ref.shape
-    rows = pl.multiple_of(pl.program_id(0) * chans, chans)
     other = jnp.concatenate([other_ref[w] for w in range(windows)], axis=1)
     total = lax.dot_general(
-        mod_ref[pl.ds(rows, chans), :],
-        other,
-        (((1,), (1,)), ((), ())),
-        preferred_element_type=jnp.float32,
-    )
-    out_ref[...] = total * scale
+        mod_ref[...], other, (((1,), (1,)), ((), ())), preferred_element_type=jnp.float32
+    )
+    for lag in range(total.shape[0] // chans):
+        rows = slice(lag * chans, (lag + 1) * chans)
+        out_ref[:, rows] = total[rows] * scale
 
 
 def correlate(mod, other, lags, scale, name):
     chans = other.shape[1]
     return pl.pallas_call(
         functools.partial(corr_kernel, scale=scale),
-        grid=(lags,),
         in_specs=[VMEM_SPEC, VMEM_SPEC],
-        out_specs=pl.BlockSpec((chans, chans), lambda lag: (0, lag)),
+        out_specs=VMEM_SPEC,
         out_shape=jax.ShapeDtypeStruct((chans, lags * chans), jnp.float32),
         name=name,
     )(in_vmem(mod), in_vmem(other))
@@ -218,9 +215,6 @@
 
     def after_own(far, own):
         return on_chip(merge_kernel, "merge", double, one(far), own)
-
-    def own_alone(white):
-        return on_chip(place_kernel, "place_own", double, one(white))
 
     def add_far(wrapped, gathered):
         return pl.pallas_call(
@@ -236,15 +230,15 @@
     own = lax.cond(at_start, one, lambda white: unwritten(single.shape, single.dtype), for_start)
     white, own = lax.optimization_barrier((white, own))
     wrapped = lax.ppermute(white, "pair", [(0, pairs - 2), (1, pairs - 1)])
+    own = lax.cond(at_end, lambda block, own: one(block), lambda block, own: own, for_end, own)
     gathered = lax.switch(
         at_start.astype(jnp.int32) + 2 * at_end.astype(jnp.int32),
         (
-            lambda for_both, for_end, far, own: both(for_both, far),
-            lambda for_both, for_end, far, own: after_own(far, own),
-            lambda for_both, for_end, far, own: own_alone(for_end),
+            lambda for_both, far, own: both(for_both, far),
+            lambda for_both, far, own: after_own(far, own),
+            lambda for_both, far, own: on_chip(place_kernel, "place_own", double, own),
         ),
         for_both,
-        for_end,
         far,
         own,
     )

time: 40.6 us -> 40.5 us (level)
  no operation moved by 1% of the time
where the time goes in v5:
time: 40.5 us; the launch traced here: 40.2 us
  blocking collectives  27.4 us (68%)
  starting transfers between devices  7.58 us (19%)
  Pallas kernels  4.33 us (11%)
  between operations  0.75 us (2%)
    all_to_all x2, blocking collectives, exchange(): return lax.all_to_all(sends, 'tm', 0, 0, tiled=True)  27.4 us
    ppermute x1, starting transfers between devices, local(): lax.ppermute(gathered[:, chans:, :], 'pair', [(p, p ^ 1) for p in range(p...  4.28 us
    ppermute x1, starting transfers between devices, gather_windows(): wrapped = lax.ppermute(white, 'pair', [(0, pairs - 2), (1, pairs - 1)])  2.01 us
    pallas_call x1, Pallas kernels, correlate_far(): pl.pallas_call(functools.partial(far_kernel, scale=scale), grid=(lags,),...  1.67 us
    ppermute x1, starting transfers between devices, gather_windows(): far = lax.ppermute(white, 'pair', [(p, p - 2) for p in range(2, pairs)])  1.29 us
    pallas_call x1, Pallas kernels, correlate(): pl.pallas_call(functools.partial(corr_kernel, scale=scale), in_specs=[VME...  1.27 us
    pallas_call x1, Pallas kernels, whiten(): pl.pallas_call(whiten_kernel, in_specs=[anywhere] * 3, out_specs=[VMEM_SP...  1.17 us
  transfers between devices with their start and end apart: 3, of which 0 were waited for; matrix products, arithmetic and copies ran while one was open for 0% of the time, Pallas kernels for 5%

profile of v5, /device:TPU:1, one launch (start us, length us, event | category | flops | bytes accessed | tf_op | source)
XLA Modules:
  0.0 40.2 jit_solution(12095268995341559424)
XLA Ops:
  0.6 1.2 %whiten.1 = (bf16[1,256,128]{2,1,0:T(8,128)(2,1)S(1)}, bf16[1,256,128]{2,1,0:T(8,128)(2,1)S(1)}, bf16[1,256,128]{2,1,0:T(8,128)(2,1)S(1)}, bf16[1,256,128]{2,1,0:T(8,128)(2,1)S(1)}) custom-call(bf16[1,256,128]{2,1,0:T(8,128)(2,1)} %raw_hbm.1, s32[1,256]{1,0:T(1,128)} %valid_hbm.1, bf16[128,128]{1,0:T(8,128)(2,1)} %constant.17.clone.basis_hbm), custom_call_target="tpu_custom_call" | custom-call | tf_op jit(solution)/shard_map/whiten/pallas_call | solution.py:70
  1.8 1.3 %collective-permute-start = (bf16[1,256,128]{2,1,0:T(8,128)(2,1)S(1)}, bf16[1,256,128]{2,1,0:T(8,128)(2,1)S(1)}, u32[]{:S(2)}, u32[]{:S(2)}) collective-permute-start(bf16[1,256,128]{2,1,0:T(8,128)(2,1)S(1)} %get-tuple-element.51), channel_id=1, source_target_pairs={{16,0},{24,8},{32,16},{40,24},{48,32},{56,40},{64,48},{72,56},{80,... | collective-permute-start | bytes 196616 | tf_op jit(solution)/shard_map/ppermute | solution.py:229
  3.1 14.1 %conditional.4 = (bf16[8,256,128]{2,1,0:T(8,128)(2,1)S(1)}) conditional(s32[]{:T(128)} %convert_element_type.10, () %tuple.37, bf16[1,256,128]{2,1,0:T(8,128)(2,1)S(1)} %get-tuple-element.48), branch_computations={%region_0.0_spmd, %region_1.0_spmd} | conditional | bytes 1048584 | solution.py:230
  3.1 0.1 spread.4
  3.2 14.0 %all_to_all.20 = bf16[8,256,128]{2,1,0:T(8,128)(2,1)S(1)} all-to-all(bf16[8,256,128]{2,1,0:T(8,128)(2,1)S(1)} %spread.4), channel_id=1, replica_groups=mesh['pair'=64,'tm'=8] {'tm'}, dimensions={0} | all-to-all | bytes 1048576 | tf_op jit(solution)/shard_map/cond/branch_1_fun/all_to_all | solution.py:208
  17.2 2.0 %collective-permute-start.1 = (bf16[1,256,128]{2,1,0:T(8,128)(2,1)S(1)}, bf16[1,256,128]{2,1,0:T(8,128)(2,1)S(1)}, u32[]{:S(2)}, u32[]{:S(2)}) collective-permute-start(bf16[1,256,128]{2,1,0:T(8,128)(2,1)S(1)} %get-tuple-element.51), channel_id=1, source_target_pairs={{0,496},{8,504},{1,497},{9,505},{2,498},{10,506},{3,499},{11,507},... | collective-permute-start | bytes 196616 | tf_op jit(solution)/shard_map/ppermute | solution.py:232
  19.2 0.0 collective-permute-done
  19.3 13.6 %conditional.6 = (bf16[8,512,128]{2,1,0:T(8,128)(2,1)S(1)}) conditional(s32[]{:T(128)} %clamp.3, (bf16[1,256,128]{2,1,0:T(8,128)(2,1)S(1)}, bf16[1,256,128]{2,1,0:T(8,128)(2,1)S(1)}) %tuple.36, (bf16[1,256,128]{2,1,0:T(8,128)(2,1)S(1)}, bf16[8,256,128]{2,1,0:T(8,128)(2,1)S(1)}) %tuple.39, ...), branch_computations={%region_4.0_spmd, %region_5.0_spmd, %region_6.0_spmd} | conditional | bytes 2097160 | solution.py:234
  19.3 0.1 spread.6
  19.4 13.4 %all_to_all.23.far_ref = bf16[8,256,128]{2,1,0:T(8,128)(2,1)S(1)} all-to-all(bf16[8,256,128]{2,1,0:T(8,128)(2,1)S(1)} %spread.6), channel_id=1, replica_groups=mesh['pair'=64,'tm'=8] {'tm'}, dimensions={0} | all-to-all | bytes 1048576 | tf_op jit(solution)/shard_map/cond/branch_1_fun/all_to_all | solution.py:208
  32.8 0.1 merge.1
  32.8 0.0 collective-permute-done.1
  32.9 0.0 copy-start
  32.9 4.3 %collective-permute-start.2 = (bf16[8,256,128]{2,1,0:T(8,128)(2,1)S(1)}, bf16[8,256,128]{2,1,0:T(8,128)(2,1)S(1)}, u32[]{:S(2)}, u32[]{:S(2)}) collective-permute-start(bf16[8,256,128]{2,1,0:T(8,128)(2,1)S(1)} %slice.4), channel_id=1, source_target_pairs={{0,8},{8,0},{16,24},{24,16},{32,40},{40,32},{48,56},{56,48},{64,72... | collective-permute-start | bytes 1572872 | tf_op jit(solution)/shard_map/ppermute | solution.py:260
  37.2 0.0 copy-done
  37.2 1.7 %far_corr.1 = (f32[256,512]{1,0:T(8,128)}, bf16[512,1024]{1,0:T(8,128)(2,1)S(1)}) custom-call(bf16[8,512,128]{2,1,0:T(8,128)(2,1)S(1)} %get-tuple-element.57.gath_ref, f32[16,256]{1,0:T(8,128)S(1)} %copy-done), custom_call_target="tpu_custom_call" | custom-call | tf_op jit(solution)/shard_map/far_corr/pallas_call | solution.py:163
  38.9 0.0 collective-permute-done.2.other_ref
  38.9 1.3 %near_corr.1 = f32[256,512]{1,0:T(8,128)} custom-call(bf16[512,1024]{1,0:T(8,128)(2,1)S(1)} %get-tuple-element.52.mod_ref, bf16[8,256,128]{2,1,0:T(8,128)(2,1)S(1)} %collective-permute-done.2.other_ref), custom_call_target="tpu_custom_call" | custom-call | tf_op jit(solution)/shard_map/near_corr/pallas_call | solution.py:189
  (3 shorter events, 0.1 us)
Async XLA Ops:
  1.8 17.4 %collective-permute-start = (bf16[1,256,128]{2,1,0:T(8,128)(2,1)S(1)}, bf16[1,256,128]{2,1,0:T(8,128)(2,1)S(1)}, u32[]{:S(2)}, u32[]{:S(2)}) collective-permute-start(bf16[1,256,128]{2,1,0:T(8,128)(2,1)S(1)} %get-tuple-element.51), channel_id=1, source_target_pairs={{16,0},{24,8},{32,16},{40,24},{48,32},{56,40},{64,48},{72,56},{80,... | collective-permute-start | bytes 196616 | tf_op jit(solution)/shard_map/ppermute | solution.py:229
  17.2 15.7 %collective-permute-start.1 = (bf16[1,256,128]{2,1,0:T(8,128)(2,1)S(1)}, bf16[1,256,128]{2,1,0:T(8,128)(2,1)S(1)}, u32[]{:S(2)}, u32[]{:S(2)}) collective-permute-start(bf16[1,256,128]{2,1,0:T(8,128)(2,1)S(1)} %get-tuple-element.51), channel_id=1, source_target_pairs={{0,496},{8,504},{1,497},{9,505},{2,498},{10,506},{3,499},{11,507},... | collective-permute-start | bytes 196616 | tf_op jit(solution)/shard_map/ppermute | solution.py:232
  32.9 4.3 %copy-start = (f32[16,256]{1,0:T(8,128)S(1)}, f32[16,256]{1,0:T(8,128)}, u32[]{:S(2)}) copy-start(f32[16,256]{1,0:T(8,128)} %constant.18.clone.table_ref) | copy-start | bytes 49156
  32.9 6.0 %collective-permute-start.2 = (bf16[8,256,128]{2,1,0:T(8,128)(2,1)S(1)}, bf16[8,256,128]{2,1,0:T(8,128)(2,1)S(1)}, u32[]{:S(2)}, u32[]{:S(2)}) collective-permute-start(bf16[8,256,128]{2,1,0:T(8,128)(2,1)S(1)} %slice.4), channel_id=1, source_target_pairs={{0,8},{8,0},{16,24},{24,16},{32,40},{40,32},{48,56},{56,48},{64,72... | collective-permute-start | bytes 1572872 | tf_op jit(solution)/shard_map/ppermute | solution.py:260

commit v6 on v5

--- a/solution.py
+++ b/solution.py
@@ -133,28 +133,32 @@
     )()
 
 
-def far_kernel(gath_ref, table_ref, out_ref, mod_ref, *, scale):
+def far_kernel(gath_ref, table_ref, out_hbm, mod_ref, out_ref, sems, *, scale):
     windows, both, width = gath_ref.shape
     chans = both // 2
-    lag = pl.program_id(0)
     own_at, far_at = slots_of(chans)
-    rows = pl.multiple_of(lag * chans, chans)
-    turn = table_ref[pl.ds(lax.axis_index("tm") * pl.num_programs(0) + lag, 1), :]
-    cos, sin = turn[:, :width], turn[:, width:]
-    for w in range(windows):
-        own = gath_ref[w, pl.ds(own_at, chans), :].astype(jnp.float32)
-        turned = own * cos + pltpu.roll(own, width // 2, 1) * sin
-        mod_ref[pl.ds(rows, chans), w * width : (w + 1) * width] = turned.astype(jnp.bfloat16)
+    lags = mod_ref.shape[0] // chans
     other = jnp.concatenate(
         [gath_ref[w, pl.ds(far_at, chans), :] for w in range(windows)], axis=1
     )
-    total = lax.dot_general(
-        mod_ref[pl.ds(rows, chans), :],
-        other,
-        (((1,), (1,)), ((), ())),
-        preferred_element_type=jnp.float32,
-    )
-    out_ref[...] = total * scale
+    turns = [table_ref[pl.ds(lax.axis_index("tm") * lags + lag, 1), :] for lag in range(lags)]
+    writes = []
+    for lag, turn in enumerate(turns):
+        rows = slice(lag * chans, (lag + 1) * chans)
+        cos, sin = turn[:, :width], turn[:, width:]
+        for w in range(windows):
+            own = gath_ref[w, pl.ds(own_at, chans), :].astype(jnp.float32)
+            turned = own * cos + pltpu.roll(own, width // 2, 1) * sin
+            mod_ref[rows, w * width : (w + 1) * width] = turned.astype(jnp.bfloat16)
+        total = lax.dot_general(
+            mod_ref[rows, :], other, (((1,), (1,)), ((), ())), preferred_element_type=jnp.float32
+        )
+        out_ref[lag] = total * scale
+        write = pltpu.make_async_copy(out_ref.at[lag], out_hbm.at[:, rows], sems.at[lag])
+        write.start()
+        writes.append(write)
+    for write in writes:
+        write.wait()
 
 
 def correlate_far(gathered, table, lags, scale):
@@ -162,12 +166,15 @@
     chans = both // 2
     return pl.pallas_call(
         functools.partial(far_kernel, scale=scale),
-        grid=(lags,),
         in_specs=[VMEM_SPEC, VMEM_SPEC],
-        out_specs=[pl.BlockSpec((chans, chans), lambda lag: (0, lag)), VMEM_SPEC],
+        out_specs=[pl.BlockSpec(memory_space=pl.ANY), VMEM_SPEC],
         out_shape=[
             jax.ShapeDtypeStruct((chans, lags * chans), jnp.float32),
             pltpu.VMEM((lags * chans, windows * width), jnp.bfloat16),
+        ],
+        scratch_shapes=[
+            pltpu.VMEM((lags, chans, chans), jnp.float32),
+            pltpu.SemaphoreType.DMA((lags,)),
         ],
         name="far_corr",
     )(in_vmem(gathered), in_vmem(table))

time: 40.5 us -> 40.3 us (level)
  transfers between devices with their start and end apart: 3 -> 3, of which waited for: 0 -> 0; matrix products, arithmetic and copies ran while one was open for 0% -> 0% of each run, Pallas kernels for 5% -> 4%
where the time goes in v6:
time: 40.3 us; the launch traced here: 40 us
  blocking collectives  27.4 us (68%)
  starting transfers between devices  7.58 us (19%)
  Pallas kernels  4.11 us (10%)
  between operations  0.76 us (2%)
    all_to_all x2, blocking collectives, exchange(): return lax.all_to_all(sends, 'tm', 0, 0, tiled=True)  27.4 us
    ppermute x1, starting transfers between devices, local(): lax.ppermute(gathered[:, chans:, :], 'pair', [(p, p ^ 1) for p in range(p...  4.28 us
    ppermute x1, starting transfers between devices, gather_windows(): wrapped = lax.ppermute(white, 'pair', [(0, pairs - 2), (1, pairs - 1)])  2.01 us
    pallas_call x1, Pallas kernels, correlate_far(): pl.pallas_call(functools.partial(far_kernel, scale=scale), in_specs=[VMEM...  1.45 us
    ppermute x1, starting transfers between devices, gather_windows(): far = lax.ppermute(white, 'pair', [(p, p - 2) for p in range(2, pairs)])  1.29 us
    pallas_call x1, Pallas kernels, correlate(): pl.pallas_call(functools.partial(corr_kernel, scale=scale), in_specs=[VME...  1.27 us
    pallas_call x1, Pallas kernels, whiten(): pl.pallas_call(whiten_kernel, in_specs=[anywhere] * 3, out_specs=[VMEM_SP...  1.17 us
  transfers between devices with their start and end apart: 3, of which 0 were waited for; matrix products, arithmetic and copies ran while one was open for 0% of the time, Pallas kernels for 4%

profile of v6, /device:TPU:1, one launch (start us, length us, event | category | flops | bytes accessed | tf_op | source)
XLA Modules:
  0.0 40.0 jit_solution(16432390487873927663)
XLA Ops:
  0.6 1.2 %whiten.1 = (bf16[1,256,128]{2,1,0:T(8,128)(2,1)S(1)}, bf16[1,256,128]{2,1,0:T(8,128)(2,1)S(1)}, bf16[1,256,128]{2,1,0:T(8,128)(2,1)S(1)}, bf16[1,256,128]{2,1,0:T(8,128)(2,1)S(1)}) custom-call(bf16[1,256,128]{2,1,0:T(8,128)(2,1)} %raw_hbm.1, s32[1,256]{1,0:T(1,128)} %valid_hbm.1, bf16[128,128]{1,0:T(8,128)(2,1)} %constant.17.clone.basis_hbm), custom_call_target="tpu_custom_call" | custom-call | tf_op jit(solution)/shard_map/whiten/pallas_call | solution.py:70
  1.8 1.3 %collective-permute-start = (bf16[1,256,128]{2,1,0:T(8,128)(2,1)S(1)}, bf16[1,256,128]{2,1,0:T(8,128)(2,1)S(1)}, u32[]{:S(2)}, u32[]{:S(2)}) collective-permute-start(bf16[1,256,128]{2,1,0:T(8,128)(2,1)S(1)} %get-tuple-element.51), channel_id=1, source_target_pairs={{16,0},{24,8},{32,16},{40,24},{48,32},{56,40},{64,48},{72,56},{80,... | collective-permute-start | bytes 196616 | tf_op jit(solution)/shard_map/ppermute | solution.py:236
  3.1 14.1 %conditional.4 = (bf16[8,256,128]{2,1,0:T(8,128)(2,1)S(1)}) conditional(s32[]{:T(128)} %convert_element_type.10, () %tuple.37, bf16[1,256,128]{2,1,0:T(8,128)(2,1)S(1)} %get-tuple-element.48), branch_computations={%region_0.0_spmd, %region_1.0_spmd} | conditional | bytes 1048584 | solution.py:237
  3.1 0.1 spread.4
  3.2 14.0 %all_to_all.20 = bf16[8,256,128]{2,1,0:T(8,128)(2,1)S(1)} all-to-all(bf16[8,256,128]{2,1,0:T(8,128)(2,1)S(1)} %spread.4), channel_id=1, replica_groups=mesh['pair'=64,'tm'=8] {'tm'}, dimensions={0} | all-to-all | bytes 1048576 | tf_op jit(solution)/shard_map/cond/branch_1_fun/all_to_all | solution.py:215
  17.2 2.0 %collective-permute-start.1 = (bf16[1,256,128]{2,1,0:T(8,128)(2,1)S(1)}, bf16[1,256,128]{2,1,0:T(8,128)(2,1)S(1)}, u32[]{:S(2)}, u32[]{:S(2)}) collective-permute-start(bf16[1,256,128]{2,1,0:T(8,128)(2,1)S(1)} %get-tuple-element.51), channel_id=1, source_target_pairs={{0,496},{8,504},{1,497},{9,505},{2,498},{10,506},{3,499},{11,507},... | collective-permute-start | bytes 196616 | tf_op jit(solution)/shard_map/ppermute | solution.py:239
  19.2 0.0 collective-permute-done
  19.3 13.6 %conditional.6 = (bf16[8,512,128]{2,1,0:T(8,128)(2,1)S(1)}) conditional(s32[]{:T(128)} %clamp.3, (bf16[1,256,128]{2,1,0:T(8,128)(2,1)S(1)}, bf16[1,256,128]{2,1,0:T(8,128)(2,1)S(1)}) %tuple.36, (bf16[1,256,128]{2,1,0:T(8,128)(2,1)S(1)}, bf16[8,256,128]{2,1,0:T(8,128)(2,1)S(1)}) %tuple.39, ...), branch_computations={%region_4.0_spmd, %region_5.0_spmd, %region_6.0_spmd} | conditional | bytes 2097160 | solution.py:241
  19.3 0.1 spread.6
  19.4 13.4 %all_to_all.23.far_ref = bf16[8,256,128]{2,1,0:T(8,128)(2,1)S(1)} all-to-all(bf16[8,256,128]{2,1,0:T(8,128)(2,1)S(1)} %spread.6), channel_id=1, replica_groups=mesh['pair'=64,'tm'=8] {'tm'}, dimensions={0} | all-to-all | bytes 1048576 | tf_op jit(solution)/shard_map/cond/branch_1_fun/all_to_all | solution.py:215
  32.8 0.1 merge.1
  32.8 0.0 collective-permute-done.1
  32.9 0.0 copy-start
  32.9 4.3 %collective-permute-start.2 = (bf16[8,256,128]{2,1,0:T(8,128)(2,1)S(1)}, bf16[8,256,128]{2,1,0:T(8,128)(2,1)S(1)}, u32[]{:S(2)}, u32[]{:S(2)}) collective-permute-start(bf16[8,256,128]{2,1,0:T(8,128)(2,1)S(1)} %slice.4), channel_id=1, source_target_pairs={{0,8},{8,0},{16,24},{24,16},{32,40},{40,32},{48,56},{56,48},{64,72... | collective-permute-start | bytes 1572872 | tf_op jit(solution)/shard_map/ppermute | solution.py:267
  37.2 0.0 copy-done
  37.2 1.4 %far_corr.1 = (f32[256,512]{1,0:T(8,128)}, bf16[512,1024]{1,0:T(8,128)(2,1)S(1)}) custom-call(bf16[8,512,128]{2,1,0:T(8,128)(2,1)S(1)} %get-tuple-element.57.gath_ref, f32[16,256]{1,0:T(8,128)S(1)} %copy-done), custom_call_target="tpu_custom_call" | custom-call | tf_op jit(solution)/shard_map/far_corr/pallas_call | solution.py:167
  38.7 0.0 collective-permute-done.2.other_ref
  38.7 1.3 %near_corr.1 = f32[256,512]{1,0:T(8,128)} custom-call(bf16[512,1024]{1,0:T(8,128)(2,1)S(1)} %get-tuple-element.52.mod_ref, bf16[8,256,128]{2,1,0:T(8,128)(2,1)S(1)} %collective-permute-done.2.other_ref), custom_call_target="tpu_custom_call" | custom-call | tf_op jit(solution)/shard_map/near_corr/pallas_call | solution.py:196
  (3 shorter events, 0.1 us)
Async XLA Ops:
  1.8 17.4 %collective-permute-start = (bf16[1,256,128]{2,1,0:T(8,128)(2,1)S(1)}, bf16[1,256,128]{2,1,0:T(8,128)(2,1)S(1)}, u32[]{:S(2)}, u32[]{:S(2)}) collective-permute-start(bf16[1,256,128]{2,1,0:T(8,128)(2,1)S(1)} %get-tuple-element.51), channel_id=1, source_target_pairs={{16,0},{24,8},{32,16},{40,24},{48,32},{56,40},{64,48},{72,56},{80,... | collective-permute-start | bytes 196616 | tf_op jit(solution)/shard_map/ppermute | solution.py:236
  17.2 15.7 %collective-permute-start.1 = (bf16[1,256,128]{2,1,0:T(8,128)(2,1)S(1)}, bf16[1,256,128]{2,1,0:T(8,128)(2,1)S(1)}, u32[]{:S(2)}, u32[]{:S(2)}) collective-permute-start(bf16[1,256,128]{2,1,0:T(8,128)(2,1)S(1)} %get-tuple-element.51), channel_id=1, source_target_pairs={{0,496},{8,504},{1,497},{9,505},{2,498},{10,506},{3,499},{11,507},... | collective-permute-start | bytes 196616 | tf_op jit(solution)/shard_map/ppermute | solution.py:239
  32.9 4.3 %copy-start = (f32[16,256]{1,0:T(8,128)S(1)}, f32[16,256]{1,0:T(8,128)}, u32[]{:S(2)}) copy-start(f32[16,256]{1,0:T(8,128)} %constant.18.clone.table_ref) | copy-start | bytes 49156
  32.9 5.8 %collective-permute-start.2 = (bf16[8,256,128]{2,1,0:T(8,128)(2,1)S(1)}, bf16[8,256,128]{2,1,0:T(8,128)(2,1)S(1)}, u32[]{:S(2)}, u32[]{:S(2)}) collective-permute-start(bf16[8,256,128]{2,1,0:T(8,128)(2,1)S(1)} %slice.4), channel_id=1, source_target_pairs={{0,8},{8,0},{16,24},{24,16},{32,40},{40,32},{48,56},{56,48},{64,72... | collective-permute-start | bytes 1572872 | tf_op jit(solution)/shard_map/ppermute | solution.py:267

commit v7 on v6

--- a/solution.py
+++ b/solution.py
@@ -122,6 +122,11 @@
     _, far_at = slots_of(chans)
     for w in range(far_ref.shape[0]):
         gath_ref[w, pl.ds(far_at, chans), :] = far_ref[w]
+
+
+def put_both_kernel(block_ref, old_ref, out_ref):
+    del old_ref
+    out_ref[...] = block_ref[...]
 
 
 def unwritten(shape, dtype):
@@ -203,11 +208,13 @@
 
 
 def gather_windows(whites, pairs, groups):
-    white, for_start, for_both, for_end = whites
+    white, for_start, for_both, for_end, for_late = whites
     windows, chans, width = white.shape
     total = windows * groups
-    at_start = lax.axis_index("pair") < 2
-    at_end = lax.axis_index("pair") >= pairs - 2
+    place = lax.axis_index("pair")
+    at_start = place < 2
+    alone = place == pairs - 2
+    at_end = jnp.logical_and(place >= pairs - 4, jnp.logical_not(alone))
     single = pltpu.VMEM((total, chans, width), white.dtype)
     double = pltpu.VMEM((total, 2 * chans, width), white.dtype)
 
@@ -223,33 +230,50 @@
     def after_own(far, own):
         return on_chip(merge_kernel, "merge", double, one(far), own)
 
-    def add_far(wrapped, gathered):
+    def put(kernel, name, block, gathered):
         return pl.pallas_call(
-            put_far_kernel,
+            kernel,
             in_specs=[VMEM_SPEC] * 2,
             out_specs=VMEM_SPEC,
             out_shape=double,
             input_output_aliases={1: 0},
-            name="put_far",
-        )(in_vmem(one(wrapped)), in_vmem(gathered))
-
-    far = lax.ppermute(white, "pair", [(p, p - 2) for p in range(2, pairs)])
+            name=name,
+        )(in_vmem(block), in_vmem(gathered))
+
+    far = lax.ppermute(white, "pair", [(p, p - 2) for p in range(2, pairs - 2)])
     own = lax.cond(at_start, one, lambda white: unwritten(single.shape, single.dtype), for_start)
     white, own = lax.optimization_barrier((white, own))
-    wrapped = lax.ppermute(white, "pair", [(0, pairs - 2), (1, pairs - 1)])
-    own = lax.cond(at_end, lambda block, own: one(block), lambda block, own: own, for_end, own)
+    wrapped = lax.ppermute(
+        white, "pair", [(p, (p - 2) % pairs) for p in (0, 1, pairs - 2, pairs - 1)]
+    )
+    own = lax.cond(alone, lambda block, own: one(block), lambda block, own: own, for_end, own)
     gathered = lax.switch(
-        at_start.astype(jnp.int32) + 2 * at_end.astype(jnp.int32),
+        at_start.astype(jnp.int32) + 2 * alone.astype(jnp.int32) + 3 * at_end.astype(jnp.int32),
         (
             lambda for_both, far, own: both(for_both, far),
             lambda for_both, far, own: after_own(far, own),
             lambda for_both, far, own: on_chip(place_kernel, "place_own", double, own),
+            lambda for_both, far, own: unwritten(double.shape, double.dtype),
         ),
         for_both,
         far,
         own,
     )
-    return lax.cond(at_end, add_far, lambda wrapped, gathered: gathered, wrapped, gathered)
+    return lax.switch(
+        alone.astype(jnp.int32) + 2 * at_end.astype(jnp.int32),
+        (
+            lambda for_late, wrapped, gathered: gathered,
+            lambda for_late, wrapped, gathered: put(
+                put_far_kernel, "put_far", one(wrapped), gathered
+            ),
+            lambda for_late, wrapped, gathered: put(
+                put_both_kernel, "put_both", both(for_late, wrapped), gathered
+            ),
+        ),
+        for_late,
+        wrapped,
+        gathered,
+    )
 
 
 def local(raw, valid):
@@ -262,7 +286,7 @@
     scale = 1.0 / math.sqrt(total * freqs)
     basis = jnp.asarray(make_basis(samples, freqs))
     table = jnp.asarray(lag_tables(LAGS, freqs, samples))
-    whites = whiten(raw, valid, basis, 4)
+    whites = whiten(raw, valid, basis, 5)
     gathered = gather_windows(whites, pairs, groups)
     near = lax.ppermute(gathered[:, chans:, :], "pair", [(p, p ^ 1) for p in range(pairs)])
     far_corr, mod = correlate_far(gathered, table, lags, scale)

time: 40.3 us -> 40.6 us (level)
  the two profiles are of different devices: /device:TPU:1 before, /device:TPU:441 now
where the time goes in v7:
time: 40.6 us; the launch traced here: 40.3 us
  starting transfers between devices  15.5 us (38%)
  blocking collectives  13.9 us (34%)
  waiting for transfers between devices  5.83 us (14%)
  Pallas kernels  4.11 us (10%)
  between operations  0.76 us (2%)
    all_to_all x1, blocking collectives, exchange(): return lax.all_to_all(sends, 'tm', 0, 0, tiled=True)  13.9 us
    ppermute x1, starting transfers between devices, local(): lax.ppermute(gathered[:, chans:, :], 'pair', [(p, p ^ 1) for p in range(p...  9.56 us
    ppermute x1, waiting for transfers between devices, gather_windows(): lax.ppermute(white, 'pair', [(p, (p - 2) % pairs) for p in (0, 1, pairs -...  5.78 us
    ppermute x1, starting transfers between devices, gather_windows(): lax.ppermute(white, 'pair', [(p, (p - 2) % pairs) for p in (0, 1, pairs -...  5.29 us
    pallas_call x1, Pallas kernels, correlate_far(): pl.pallas_call(functools.partial(far_kernel, scale=scale), in_specs=[VMEM...  1.45 us
    pallas_call x1, Pallas kernels, correlate(): pl.pallas_call(functools.partial(corr_kernel, scale=scale), in_specs=[VME...  1.27 us
    pallas_call x1, Pallas kernels, whiten(): pl.pallas_call(whiten_kernel, in_specs=[anywhere] * 3, out_specs=[VMEM_SP...  1.18 us
  transfers between devices with their start and end apart: 3, of which 1 were waited for; matrix products, arithmetic and copies ran while one was open for 0% of the time, Pallas kernels for 4%

profile of v7, /device:TPU:441, one launch (start us, length us, event | category | flops | bytes accessed | tf_op | source)
XLA Modules:
  0.0 40.3 jit_solution(8273336787258313455)
XLA Ops:
  0.6 1.2 %whiten.1 = (bf16[1,256,128]{2,1,0:T(8,128)(2,1)S(1)}, bf16[1,256,128]{2,1,0:T(8,128)(2,1)S(1)}, bf16[1,256,128]{2,1,0:T(8,128)(2,1)S(1)}, bf16[1,256,128]{2,1,0:T(8,128)(2,1)S(1)}, bf16[1,256,128]{2,1,0:T(8,128)(2,1)S(1)}) custom-call(bf16[1,256,128]{2,1,0:T(8,128)(2,1)} %raw_hbm.1, s32[1,256]{1,0:T(1,128)} %valid_hbm.1, ...), custom_call_target="tpu_custom_call" | custom-call | tf_op jit(solution)/shard_map/whiten/pallas_call | solution.py:70
  1.8 0.7 %collective-permute-start = (bf16[1,256,128]{2,1,0:T(8,128)(2,1)S(1)}, bf16[1,256,128]{2,1,0:T(8,128)(2,1)S(1)}, u32[]{:S(2)}, u32[]{:S(2)}) collective-permute-start(bf16[1,256,128]{2,1,0:T(8,128)(2,1)S(1)} %get-tuple-element.63), channel_id=1, source_target_pairs={{16,0},{24,8},{32,16},{40,24},{48,32},{56,40},{64,48},{72,56},{80,... | collective-permute-start | bytes 196616 | tf_op jit(solution)/shard_map/ppermute | solution.py:243
  2.5 5.3 %collective-permute-start.1 = (bf16[1,256,128]{2,1,0:T(8,128)(2,1)S(1)}, bf16[1,256,128]{2,1,0:T(8,128)(2,1)S(1)}, u32[]{:S(2)}, u32[]{:S(2)}) collective-permute-start(bf16[1,256,128]{2,1,0:T(8,128)(2,1)S(1)} %get-tuple-element.63), channel_id=1, source_target_pairs={{0,496},{8,504},{496,480},{504,488},{1,497},{9,505},{497,481},{505... | collective-permute-start | bytes 196616 | tf_op jit(solution)/shard_map/ppermute | solution.py:246
  7.9 0.0 collective-permute-done
  7.9 5.8 %collective-permute-done.1 = bf16[1,256,128]{2,1,0:T(8,128)(2,1)S(1)} collective-permute-done((bf16[1,256,128]{2,1,0:T(8,128)(2,1)S(1)}, bf16[1,256,128]{2,1,0:T(8,128)(2,1)S(1)}, u32[]{:S(2)}, u32[]{:S(2)}) %collective-permute-start.1) | collective-permute-done | bytes 65568 | tf_op jit(solution)/shard_map/ppermute | solution.py:246
  13.7 14.2 %conditional.7 = (bf16[8,512,128]{2,1,0:T(8,128)(2,1)S(1)}) conditional(s32[]{:T(128)} %clamp.6, bf16[8,512,128]{2,1,0:T(8,128)(2,1)S(1)} %get-tuple-element.69, (bf16[1,256,128]{2,1,0:T(8,128)(2,1)S(1)}, bf16[8,512,128]{2,1,0:T(8,128)(2,1)S(1)}) %tuple.47, (bf16[1,256,128]{2,1,0:T(8,128)(2,1)S(1)}, ...), branch_computations={%region_8.0_spmd, %region_9.0_spmd, %region_10.0_spmd} | conditional | bytes 2097160 | solution.py:262
  13.7 0.1 slots.3
  13.8 13.9 %all_to_all.29.block_ref = bf16[8,512,128]{2,1,0:T(8,128)(2,1)S(1)} all-to-all(bf16[8,512,128]{2,1,0:T(8,128)(2,1)S(1)} %slots.3), channel_id=1, replica_groups=mesh['pair'=64,'tm'=8] {'tm'}, dimensions={0} | all-to-all | bytes 2097152 | tf_op jit(solution)/shard_map/cond/branch_2_fun/all_to_all | solution.py:222
  27.8 0.1 put_both.1
  27.9 0.0 copy-start
  27.9 9.6 %collective-permute-start.2 = (bf16[8,256,128]{2,1,0:T(8,128)(2,1)S(1)}, bf16[8,256,128]{2,1,0:T(8,128)(2,1)S(1)}, u32[]{:S(2)}, u32[]{:S(2)}) collective-permute-start(bf16[8,256,128]{2,1,0:T(8,128)(2,1)S(1)} %slice.4), channel_id=1, source_target_pairs={{0,8},{8,0},{16,24},{24,16},{32,40},{40,32},{48,56},{56,48},{64,72... | collective-permute-start | bytes 1572872 | tf_op jit(solution)/shard_map/ppermute | solution.py:291
  37.5 0.0 copy-done
  37.5 1.4 %far_corr.1 = (f32[256,512]{1,0:T(8,128)}, bf16[512,1024]{1,0:T(8,128)(2,1)S(1)}) custom-call(bf16[8,512,128]{2,1,0:T(8,128)(2,1)S(1)} %get-tuple-element.70.gath_ref, f32[16,256]{1,0:T(8,128)S(1)} %copy-done), custom_call_target="tpu_custom_call" | custom-call | tf_op jit(solution)/shard_map/far_corr/pallas_call | solution.py:172
  39.0 0.0 collective-permute-done.2.other_ref
  39.0 1.3 %near_corr.1 = f32[256,512]{1,0:T(8,128)} custom-call(bf16[512,1024]{1,0:T(8,128)(2,1)S(1)} %get-tuple-element.65.mod_ref, bf16[8,256,128]{2,1,0:T(8,128)(2,1)S(1)} %collective-permute-done.2.other_ref), custom_call_target="tpu_custom_call" | custom-call | tf_op jit(solution)/shard_map/near_corr/pallas_call | solution.py:201
  (6 shorter events, 0.1 us)
Async XLA Ops:
  1.8 6.0 %collective-permute-start = (bf16[1,256,128]{2,1,0:T(8,128)(2,1)S(1)}, bf16[1,256,128]{2,1,0:T(8,128)(2,1)S(1)}, u32[]{:S(2)}, u32[]{:S(2)}) collective-permute-start(bf16[1,256,128]{2,1,0:T(8,128)(2,1)S(1)} %get-tuple-element.63), channel_id=1, source_target_pairs={{16,0},{24,8},{32,16},{40,24},{48,32},{56,40},{64,48},{72,56},{80,... | collective-permute-start | bytes 196616 | tf_op jit(solution)/shard_map/ppermute | solution.py:243
  2.5 11.2 %collective-permute-start.1 = (bf16[1,256,128]{2,1,0:T(8,128)(2,1)S(1)}, bf16[1,256,128]{2,1,0:T(8,128)(2,1)S(1)}, u32[]{:S(2)}, u32[]{:S(2)}) collective-permute-start(bf16[1,256,128]{2,1,0:T(8,128)(2,1)S(1)} %get-tuple-element.63), channel_id=1, source_target_pairs={{0,496},{8,504},{496,480},{504,488},{1,497},{9,505},{497,481},{505... | collective-permute-start | bytes 196616 | tf_op jit(solution)/shard_map/ppermute | solution.py:246
  27.9 9.6 %copy-start = (f32[16,256]{1,0:T(8,128)S(1)}, f32[16,256]{1,0:T(8,128)}, u32[]{:S(2)}) copy-start(f32[16,256]{1,0:T(8,128)} %constant.24.clone.table_ref) | copy-start | bytes 49156
  27.9 11.1 %collective-permute-start.2 = (bf16[8,256,128]{2,1,0:T(8,128)(2,1)S(1)}, bf16[8,256,128]{2,1,0:T(8,128)(2,1)S(1)}, u32[]{:S(2)}, u32[]{:S(2)}) collective-permute-start(bf16[8,256,128]{2,1,0:T(8,128)(2,1)S(1)} %slice.4), channel_id=1, source_target_pairs={{0,8},{8,0},{16,24},{24,16},{32,40},{40,32},{48,56},{56,48},{64,72... | collective-permute-start | bytes 1572872 | tf_op jit(solution)/shard_map/ppermute | solution.py:291

commit v8 on v7

--- a/solution.py
+++ b/solution.py
@@ -106,21 +106,6 @@
     own_at, far_at = slots_of(chans)
     for w in range(far_ref.shape[0]):
         gath_ref[w, pl.ds(own_at, chans), :] = early_ref[w]
-        gath_ref[w, pl.ds(far_at, chans), :] = far_ref[w]
-
-
-def place_kernel(own_ref, gath_ref):
-    chans = own_ref.shape[1]
-    own_at, _ = slots_of(chans)
-    for w in range(own_ref.shape[0]):
-        gath_ref[w, pl.ds(own_at, chans), :] = own_ref[w]
-
-
-def put_far_kernel(far_ref, old_ref, gath_ref):
-    del old_ref
-    chans = far_ref.shape[1]
-    _, far_at = slots_of(chans)
-    for w in range(far_ref.shape[0]):
         gath_ref[w, pl.ds(far_at, chans), :] = far_ref[w]
 
 
@@ -208,13 +193,12 @@
 
 
 def gather_windows(whites, pairs, groups):
-    white, for_start, for_both, for_end, for_late = whites
+    white, for_start, for_both, for_late = whites
     windows, chans, width = white.shape
     total = windows * groups
     place = lax.axis_index("pair")
     at_start = place < 2
-    alone = place == pairs - 2
-    at_end = jnp.logical_and(place >= pairs - 4, jnp.logical_not(alone))
+    at_end = place >= pairs - 4
     single = pltpu.VMEM((total, chans, width), white.dtype)
     double = pltpu.VMEM((total, 2 * chans, width), white.dtype)
 
@@ -230,14 +214,14 @@
     def after_own(far, own):
         return on_chip(merge_kernel, "merge", double, one(far), own)
 
-    def put(kernel, name, block, gathered):
+    def put(block, gathered):
         return pl.pallas_call(
-            kernel,
+            put_both_kernel,
             in_specs=[VMEM_SPEC] * 2,
             out_specs=VMEM_SPEC,
             out_shape=double,
             input_output_aliases={1: 0},
-            name=name,
+            name="put_both",
         )(in_vmem(block), in_vmem(gathered))
 
     far = lax.ppermute(white, "pair", [(p, p - 2) for p in range(2, pairs - 2)])
@@ -246,30 +230,21 @@
     wrapped = lax.ppermute(
         white, "pair", [(p, (p - 2) % pairs) for p in (0, 1, pairs - 2, pairs - 1)]
     )
-    own = lax.cond(alone, lambda block, own: one(block), lambda block, own: own, for_end, own)
     gathered = lax.switch(
-        at_start.astype(jnp.int32) + 2 * alone.astype(jnp.int32) + 3 * at_end.astype(jnp.int32),
+        at_start.astype(jnp.int32) + 2 * at_end.astype(jnp.int32),
         (
             lambda for_both, far, own: both(for_both, far),
             lambda for_both, far, own: after_own(far, own),
-            lambda for_both, far, own: on_chip(place_kernel, "place_own", double, own),
             lambda for_both, far, own: unwritten(double.shape, double.dtype),
         ),
         for_both,
         far,
         own,
     )
-    return lax.switch(
-        alone.astype(jnp.int32) + 2 * at_end.astype(jnp.int32),
-        (
-            lambda for_late, wrapped, gathered: gathered,
-            lambda for_late, wrapped, gathered: put(
-                put_far_kernel, "put_far", one(wrapped), gathered
-            ),
-            lambda for_late, wrapped, gathered: put(
-                put_both_kernel, "put_both", both(for_late, wrapped), gathered
-            ),
-        ),
+    return lax.cond(
+        at_end,
+        lambda for_late, wrapped, gathered: put(both(for_late, wrapped), gathered),
+        lambda for_late, wrapped, gathered: gathered,
         for_late,
         wrapped,
         gathered,
@@ -286,7 +261,7 @@
     scale = 1.0 / math.sqrt(total * freqs)
     basis = jnp.asarray(make_basis(samples, freqs))
     table = jnp.asarray(lag_tables(LAGS, freqs, samples))
-    whites = whiten(raw, valid, basis, 5)
+    whites = whiten(raw, valid, basis, 4)
     gathered = gather_windows(whites, pairs, groups)
     near = lax.ppermute(gathered[:, chans:, :], "pair", [(p, p ^ 1) for p in range(pairs)])
     far_corr, mod = correlate_far(gathered, table, lags, scale)

time: 40.6 us -> 39 us (0.961)
  the two profiles are of different devices: /device:TPU:441 before, /device:TPU:1 now
where the time goes in v8:
time: 39 us; the launch traced here: 38.7 us
  blocking collectives  24.7 us (63%)
  starting transfers between devices  8.97 us (23%)
  Pallas kernels  4.11 us (11%)
  between operations  0.75 us (2%)
    all_to_all x2, blocking collectives, exchange(): return lax.all_to_all(sends, 'tm', 0, 0, tiled=True)  24.7 us
    ppermute x1, starting transfers between devices, local(): lax.ppermute(gathered[:, chans:, :], 'pair', [(p, p ^ 1) for p in range(p...  6.39 us
    pallas_call x1, Pallas kernels, correlate_far(): pl.pallas_call(functools.partial(far_kernel, scale=scale), in_specs=[VMEM...  1.45 us
    ppermute x1, starting transfers between devices, gather_windows(): far = lax.ppermute(white, 'pair', [(p, p - 2) for p in range(2, pairs - 2)])  1.29 us
    ppermute x1, starting transfers between devices, gather_windows(): lax.ppermute(white, 'pair', [(p, (p - 2) % pairs) for p in (0, 1, pairs -...  1.28 us
    pallas_call x1, Pallas kernels, correlate(): pl.pallas_call(functools.partial(corr_kernel, scale=scale), in_specs=[VME...  1.27 us
    pallas_call x1, Pallas kernels, whiten(): pl.pallas_call(whiten_kernel, in_specs=[anywhere] * 3, out_specs=[VMEM_SP...  1.17 us
  transfers between devices with their start and end apart: 3, of which 0 were waited for; matrix products, arithmetic and copies ran while one was open for 0% of the time, Pallas kernels for 4%

profile of v8, /device:TPU:1, one launch (start us, length us, event | category | flops | bytes accessed | tf_op | source)
XLA Modules:
  0.0 38.7 jit_solution(8624429124421106170)
XLA Ops:
  0.6 1.2 %whiten.1 = (bf16[1,256,128]{2,1,0:T(8,128)(2,1)S(1)}, bf16[1,256,128]{2,1,0:T(8,128)(2,1)S(1)}, bf16[1,256,128]{2,1,0:T(8,128)(2,1)S(1)}, bf16[1,256,128]{2,1,0:T(8,128)(2,1)S(1)}) custom-call(bf16[1,256,128]{2,1,0:T(8,128)(2,1)} %raw_hbm.1, s32[1,256]{1,0:T(1,128)} %valid_hbm.1, bf16[128,128]{1,0:T(8,128)(2,1)} %constant.17.clone.basis_hbm), custom_call_target="tpu_custom_call" | custom-call | tf_op jit(solution)/shard_map/whiten/pallas_call | solution.py:70
  1.8 1.3 %collective-permute-start = (bf16[1,256,128]{2,1,0:T(8,128)(2,1)S(1)}, bf16[1,256,128]{2,1,0:T(8,128)(2,1)S(1)}, u32[]{:S(2)}, u32[]{:S(2)}) collective-permute-start(bf16[1,256,128]{2,1,0:T(8,128)(2,1)S(1)} %get-tuple-element.48), channel_id=1, source_target_pairs={{16,0},{24,8},{32,16},{40,24},{48,32},{56,40},{64,48},{72,56},{80,... | collective-permute-start | bytes 196616 | tf_op jit(solution)/shard_map/ppermute | solution.py:227
  3.1 14.1 %conditional.3 = (bf16[8,256,128]{2,1,0:T(8,128)(2,1)S(1)}) conditional(s32[]{:T(128)} %convert_element_type.9, () %tuple.31, bf16[1,256,128]{2,1,0:T(8,128)(2,1)S(1)} %get-tuple-element.45), branch_computations={%region_0.0_spmd, %region_1.0_spmd} | conditional | bytes 1048584 | solution.py:228
  3.1 0.1 spread.2
  3.2 14.0 %all_to_all.16 = bf16[8,256,128]{2,1,0:T(8,128)(2,1)S(1)} all-to-all(bf16[8,256,128]{2,1,0:T(8,128)(2,1)S(1)} %spread.2), channel_id=1, replica_groups=mesh['pair'=64,'tm'=8] {'tm'}, dimensions={0} | all-to-all | bytes 1048576 | tf_op jit(solution)/shard_map/cond/branch_1_fun/all_to_all | solution.py:206
  17.2 1.3 %collective-permute-start.1 = (bf16[1,256,128]{2,1,0:T(8,128)(2,1)S(1)}, bf16[1,256,128]{2,1,0:T(8,128)(2,1)S(1)}, u32[]{:S(2)}, u32[]{:S(2)}) collective-permute-start(bf16[1,256,128]{2,1,0:T(8,128)(2,1)S(1)} %get-tuple-element.48), channel_id=1, source_target_pairs={{0,496},{8,504},{496,480},{504,488},{1,497},{9,505},{497,481},{505... | collective-permute-start | bytes 196616 | tf_op jit(solution)/shard_map/ppermute | solution.py:230
  18.5 0.0 collective-permute-done
  18.5 10.9 %conditional.4 = (bf16[8,512,128]{2,1,0:T(8,128)(2,1)S(1)}) conditional(s32[]{:T(128)} %clamp.3, (bf16[1,256,128]{2,1,0:T(8,128)(2,1)S(1)}, bf16[1,256,128]{2,1,0:T(8,128)(2,1)S(1)}) %tuple.30, (bf16[1,256,128]{2,1,0:T(8,128)(2,1)S(1)}, bf16[8,256,128]{2,1,0:T(8,128)(2,1)S(1)}) %tuple.33, () %tuple.34), branch_computations={%region_2.0_spmd, %region_3.0_spmd, %region_4.0_spmd} | conditional | bytes 2097160 | solution.py:233
  18.5 0.1 spread.3
  18.6 10.7 %all_to_all.18.far_ref = bf16[8,256,128]{2,1,0:T(8,128)(2,1)S(1)} all-to-all(bf16[8,256,128]{2,1,0:T(8,128)(2,1)S(1)} %spread.3), channel_id=1, replica_groups=mesh['pair'=64,'tm'=8] {'tm'}, dimensions={0} | all-to-all | bytes 1048576 | tf_op jit(solution)/shard_map/cond/branch_1_fun/all_to_all | solution.py:206
  29.3 0.1 merge.1
  29.4 0.0 collective-permute-done.1
  29.4 0.0 copy-start
  29.5 6.4 %collective-permute-start.2 = (bf16[8,256,128]{2,1,0:T(8,128)(2,1)S(1)}, bf16[8,256,128]{2,1,0:T(8,128)(2,1)S(1)}, u32[]{:S(2)}, u32[]{:S(2)}) collective-permute-start(bf16[8,256,128]{2,1,0:T(8,128)(2,1)S(1)} %slice.4), channel_id=1, source_target_pairs={{0,8},{8,0},{16,24},{24,16},{32,40},{40,32},{48,56},{56,48},{64,72... | collective-permute-start | bytes 1572872 | tf_op jit(solution)/shard_map/ppermute | solution.py:266
  35.9 0.0 copy-done
  35.9 1.4 %far_corr.1 = (f32[256,512]{1,0:T(8,128)}, bf16[512,1024]{1,0:T(8,128)(2,1)S(1)}) custom-call(bf16[8,512,128]{2,1,0:T(8,128)(2,1)S(1)} %get-tuple-element.53.gath_ref, f32[16,256]{1,0:T(8,128)S(1)} %copy-done), custom_call_target="tpu_custom_call" | custom-call | tf_op jit(solution)/shard_map/far_corr/pallas_call | solution.py:157
  37.3 0.0 collective-permute-done.2.other_ref
  37.4 1.3 %near_corr.1 = f32[256,512]{1,0:T(8,128)} custom-call(bf16[512,1024]{1,0:T(8,128)(2,1)S(1)} %get-tuple-element.49.mod_ref, bf16[8,256,128]{2,1,0:T(8,128)(2,1)S(1)} %collective-permute-done.2.other_ref), custom_call_target="tpu_custom_call" | custom-call | tf_op jit(solution)/shard_map/near_corr/pallas_call | solution.py:186
  (2 shorter events, 0.0 us)
Async XLA Ops:
  1.8 16.7 %collective-permute-start = (bf16[1,256,128]{2,1,0:T(8,128)(2,1)S(1)}, bf16[1,256,128]{2,1,0:T(8,128)(2,1)S(1)}, u32[]{:S(2)}, u32[]{:S(2)}) collective-permute-start(bf16[1,256,128]{2,1,0:T(8,128)(2,1)S(1)} %get-tuple-element.48), channel_id=1, source_target_pairs={{16,0},{24,8},{32,16},{40,24},{48,32},{56,40},{64,48},{72,56},{80,... | collective-permute-start | bytes 196616 | tf_op jit(solution)/shard_map/ppermute | solution.py:227
  17.2 12.2 %collective-permute-start.1 = (bf16[1,256,128]{2,1,0:T(8,128)(2,1)S(1)}, bf16[1,256,128]{2,1,0:T(8,128)(2,1)S(1)}, u32[]{:S(2)}, u32[]{:S(2)}) collective-permute-start(bf16[1,256,128]{2,1,0:T(8,128)(2,1)S(1)} %get-tuple-element.48), channel_id=1, source_target_pairs={{0,496},{8,504},{496,480},{504,488},{1,497},{9,505},{497,481},{505... | collective-permute-start | bytes 196616 | tf_op jit(solution)/shard_map/ppermute | solution.py:230
  29.4 6.5 %copy-start = (f32[16,256]{1,0:T(8,128)S(1)}, f32[16,256]{1,0:T(8,128)}, u32[]{:S(2)}) copy-start(f32[16,256]{1,0:T(8,128)} %constant.18.clone.table_ref) | copy-start | bytes 49156
  29.5 7.9 %collective-permute-start.2 = (bf16[8,256,128]{2,1,0:T(8,128)(2,1)S(1)}, bf16[8,256,128]{2,1,0:T(8,128)(2,1)S(1)}, u32[]{:S(2)}, u32[]{:S(2)}) collective-permute-start(bf16[8,256,128]{2,1,0:T(8,128)(2,1)S(1)} %slice.4), channel_id=1, source_target_pairs={{0,8},{8,0},{16,24},{24,16},{32,40},{40,32},{48,56},{56,48},{64,72... | collective-permute-start | bytes 1572872 | tf_op jit(solution)/shard_map/ppermute | solution.py:266

commit v9 on v8

--- a/solution.py
+++ b/solution.py
@@ -170,15 +170,21 @@
     )(in_vmem(gathered), in_vmem(table))
 
 
-def corr_kernel(mod_ref, other_ref, out_ref, *, scale):
+def corr_kernel(mod_ref, other_ref, out_hbm, out_ref, sems, *, scale):
     windows, chans, _ = other_ref.shape
     other = jnp.concatenate([other_ref[w] for w in range(windows)], axis=1)
     total = lax.dot_general(
         mod_ref[...], other, (((1,), (1,)), ((), ())), preferred_element_type=jnp.float32
     )
+    writes = []
     for lag in range(total.shape[0] // chans):
         rows = slice(lag * chans, (lag + 1) * chans)
-        out_ref[:, rows] = total[rows] * scale
+        out_ref[lag] = total[rows] * scale
+        write = pltpu.make_async_copy(out_ref.at[lag], out_hbm.at[:, rows], sems.at[lag])
+        write.start()
+        writes.append(write)
+    for write in writes:
+        write.wait()
 
 
 def correlate(mod, other, lags, scale, name):
@@ -186,8 +192,12 @@
     return pl.pallas_call(
         functools.partial(corr_kernel, scale=scale),
         in_specs=[VMEM_SPEC, VMEM_SPEC],
-        out_specs=VMEM_SPEC,
+        out_specs=pl.BlockSpec(memory_space=pl.ANY),
         out_shape=jax.ShapeDtypeStruct((chans, lags * chans), jnp.float32),
+        scratch_shapes=[
+            pltpu.VMEM((lags, chans, chans), jnp.float32),
+            pltpu.SemaphoreType.DMA((lags,)),
+        ],
         name=name,
     )(in_vmem(mod), in_vmem(other))
 

time: 39 us -> 38.9 us (level)
  no operation moved by 1% of the time
where the time goes in v9:
time: 38.9 us; the launch traced here: 38.6 us
  blocking collectives  24.7 us (63%)
  starting transfers between devices  8.97 us (23%)
  Pallas kernels  4.05 us (10%)
  between operations  0.75 us (2%)
    all_to_all x2, blocking collectives, exchange(): return lax.all_to_all(sends, 'tm', 0, 0, tiled=True)  24.7 us
    ppermute x1, starting transfers between devices, local(): lax.ppermute(gathered[:, chans:, :], 'pair', [(p, p ^ 1) for p in range(p...  6.39 us
    pallas_call x1, Pallas kernels, correlate_far(): pl.pallas_call(functools.partial(far_kernel, scale=scale), in_specs=[VMEM...  1.45 us
    ppermute x1, starting transfers between devices, gather_windows(): far = lax.ppermute(white, 'pair', [(p, p - 2) for p in range(2, pairs - 2)])  1.29 us
    ppermute x1, starting transfers between devices, gather_windows(): lax.ppermute(white, 'pair', [(p, (p - 2) % pairs) for p in (0, 1, pairs -...  1.28 us
    pallas_call x1, Pallas kernels, correlate(): pl.pallas_call(functools.partial(corr_kernel, scale=scale), in_specs=[VME...  1.21 us
    pallas_call x1, Pallas kernels, whiten(): pl.pallas_call(whiten_kernel, in_specs=[anywhere] * 3, out_specs=[VMEM_SP...  1.17 us
  transfers between devices with their start and end apart: 3, of which 0 were waited for; matrix products, arithmetic and copies ran while one was open for 0% of the time, Pallas kernels for 4%

profile of v9, /device:TPU:1, one launch (start us, length us, event | category | flops | bytes accessed | tf_op | source)
XLA Modules:
  0.0 38.6 jit_solution(8071134725122318431)
XLA Ops:
  0.6 1.2 %whiten.1 = (bf16[1,256,128]{2,1,0:T(8,128)(2,1)S(1)}, bf16[1,256,128]{2,1,0:T(8,128)(2,1)S(1)}, bf16[1,256,128]{2,1,0:T(8,128)(2,1)S(1)}, bf16[1,256,128]{2,1,0:T(8,128)(2,1)S(1)}) custom-call(bf16[1,256,128]{2,1,0:T(8,128)(2,1)} %raw_hbm.1, s32[1,256]{1,0:T(1,128)} %valid_hbm.1, bf16[128,128]{1,0:T(8,128)(2,1)} %constant.17.clone.basis_hbm), custom_call_target="tpu_custom_call" | custom-call | tf_op jit(solution)/shard_map/whiten/pallas_call | solution.py:70
  1.8 1.3 %collective-permute-start = (bf16[1,256,128]{2,1,0:T(8,128)(2,1)S(1)}, bf16[1,256,128]{2,1,0:T(8,128)(2,1)S(1)}, u32[]{:S(2)}, u32[]{:S(2)}) collective-permute-start(bf16[1,256,128]{2,1,0:T(8,128)(2,1)S(1)} %get-tuple-element.48), channel_id=1, source_target_pairs={{16,0},{24,8},{32,16},{40,24},{48,32},{56,40},{64,48},{72,56},{80,... | collective-permute-start | bytes 196616 | tf_op jit(solution)/shard_map/ppermute | solution.py:237
  3.1 14.1 %conditional.3 = (bf16[8,256,128]{2,1,0:T(8,128)(2,1)S(1)}) conditional(s32[]{:T(128)} %convert_element_type.9, () %tuple.31, bf16[1,256,128]{2,1,0:T(8,128)(2,1)S(1)} %get-tuple-element.45), branch_computations={%region_0.0_spmd, %region_1.0_spmd} | conditional | bytes 1048584 | solution.py:238
  3.1 0.1 spread.2
  3.2 14.0 %all_to_all.16 = bf16[8,256,128]{2,1,0:T(8,128)(2,1)S(1)} all-to-all(bf16[8,256,128]{2,1,0:T(8,128)(2,1)S(1)} %spread.2), channel_id=1, replica_groups=mesh['pair'=64,'tm'=8] {'tm'}, dimensions={0} | all-to-all | bytes 1048576 | tf_op jit(solution)/shard_map/cond/branch_1_fun/all_to_all | solution.py:216
  17.2 1.3 %collective-permute-start.1 = (bf16[1,256,128]{2,1,0:T(8,128)(2,1)S(1)}, bf16[1,256,128]{2,1,0:T(8,128)(2,1)S(1)}, u32[]{:S(2)}, u32[]{:S(2)}) collective-permute-start(bf16[1,256,128]{2,1,0:T(8,128)(2,1)S(1)} %get-tuple-element.48), channel_id=1, source_target_pairs={{0,496},{8,504},{496,480},{504,488},{1,497},{9,505},{497,481},{505... | collective-permute-start | bytes 196616 | tf_op jit(solution)/shard_map/ppermute | solution.py:240
  18.5 0.0 collective-permute-done
  18.5 10.9 %conditional.4 = (bf16[8,512,128]{2,1,0:T(8,128)(2,1)S(1)}) conditional(s32[]{:T(128)} %clamp.3, (bf16[1,256,128]{2,1,0:T(8,128)(2,1)S(1)}, bf16[1,256,128]{2,1,0:T(8,128)(2,1)S(1)}) %tuple.30, (bf16[1,256,128]{2,1,0:T(8,128)(2,1)S(1)}, bf16[8,256,128]{2,1,0:T(8,128)(2,1)S(1)}) %tuple.33, () %tuple.34), branch_computations={%region_2.0_spmd, %region_3.0_spmd, %region_4.0_spmd} | conditional | bytes 2097160 | solution.py:243
  18.5 0.1 spread.3
  18.6 10.7 %all_to_all.18.far_ref = bf16[8,256,128]{2,1,0:T(8,128)(2,1)S(1)} all-to-all(bf16[8,256,128]{2,1,0:T(8,128)(2,1)S(1)} %spread.3), channel_id=1, replica_groups=mesh['pair'=64,'tm'=8] {'tm'}, dimensions={0} | all-to-all | bytes 1048576 | tf_op jit(solution)/shard_map/cond/branch_1_fun/all_to_all | solution.py:216
  29.3 0.1 merge.1
  29.4 0.0 collective-permute-done.1
  29.4 0.0 copy-start
  29.5 6.4 %collective-permute-start.2 = (bf16[8,256,128]{2,1,0:T(8,128)(2,1)S(1)}, bf16[8,256,128]{2,1,0:T(8,128)(2,1)S(1)}, u32[]{:S(2)}, u32[]{:S(2)}) collective-permute-start(bf16[8,256,128]{2,1,0:T(8,128)(2,1)S(1)} %slice.4), channel_id=1, source_target_pairs={{0,8},{8,0},{16,24},{24,16},{32,40},{40,32},{48,56},{56,48},{64,72... | collective-permute-start | bytes 1572872 | tf_op jit(solution)/shard_map/ppermute | solution.py:276
  35.9 0.0 copy-done
  35.9 1.4 %far_corr.1 = (f32[256,512]{1,0:T(8,128)}, bf16[512,1024]{1,0:T(8,128)(2,1)S(1)}) custom-call(bf16[8,512,128]{2,1,0:T(8,128)(2,1)S(1)} %get-tuple-element.53.gath_ref, f32[16,256]{1,0:T(8,128)S(1)} %copy-done), custom_call_target="tpu_custom_call" | custom-call | tf_op jit(solution)/shard_map/far_corr/pallas_call | solution.py:157
  37.3 0.0 collective-permute-done.2.other_ref
  37.4 1.2 %near_corr.1 = f32[256,512]{1,0:T(8,128)} custom-call(bf16[512,1024]{1,0:T(8,128)(2,1)S(1)} %get-tuple-element.49.mod_ref, bf16[8,256,128]{2,1,0:T(8,128)(2,1)S(1)} %collective-permute-done.2.other_ref), custom_call_target="tpu_custom_call" | custom-call | tf_op jit(solution)/shard_map/near_corr/pallas_call | solution.py:192
  (2 shorter events, 0.0 us)
Async XLA Ops:
  1.8 16.7 %collective-permute-start = (bf16[1,256,128]{2,1,0:T(8,128)(2,1)S(1)}, bf16[1,256,128]{2,1,0:T(8,128)(2,1)S(1)}, u32[]{:S(2)}, u32[]{:S(2)}) collective-permute-start(bf16[1,256,128]{2,1,0:T(8,128)(2,1)S(1)} %get-tuple-element.48), channel_id=1, source_target_pairs={{16,0},{24,8},{32,16},{40,24},{48,32},{56,40},{64,48},{72,56},{80,... | collective-permute-start | bytes 196616 | tf_op jit(solution)/shard_map/ppermute | solution.py:237
  17.2 12.2 %collective-permute-start.1 = (bf16[1,256,128]{2,1,0:T(8,128)(2,1)S(1)}, bf16[1,256,128]{2,1,0:T(8,128)(2,1)S(1)}, u32[]{:S(2)}, u32[]{:S(2)}) collective-permute-start(bf16[1,256,128]{2,1,0:T(8,128)(2,1)S(1)} %get-tuple-element.48), channel_id=1, source_target_pairs={{0,496},{8,504},{496,480},{504,488},{1,497},{9,505},{497,481},{505... | collective-permute-start | bytes 196616 | tf_op jit(solution)/shard_map/ppermute | solution.py:240
  29.4 6.5 %copy-start = (f32[16,256]{1,0:T(8,128)S(1)}, f32[16,256]{1,0:T(8,128)}, u32[]{:S(2)}) copy-start(f32[16,256]{1,0:T(8,128)} %constant.18.clone.table_ref) | copy-start | bytes 49156
  29.5 7.9 %collective-permute-start.2 = (bf16[8,256,128]{2,1,0:T(8,128)(2,1)S(1)}, bf16[8,256,128]{2,1,0:T(8,128)(2,1)S(1)}, u32[]{:S(2)}, u32[]{:S(2)}) collective-permute-start(bf16[8,256,128]{2,1,0:T(8,128)(2,1)S(1)} %slice.4), channel_id=1, source_target_pairs={{0,8},{8,0},{16,24},{24,16},{32,40},{40,32},{48,56},{56,48},{64,72... | collective-permute-start | bytes 1572872 | tf_op jit(solution)/shard_map/ppermute | solution.py:276
